TPU v7x, 512 devices: a whole 4x4x16 slice. The times are simulated.
512 devices in a mesh: cfg: 2 (over x_lo), seq: 256 (over y, x_hi, z, core).
Axes of the slice: x: 4 (x_hi: 2, x_lo: 2; x = x_hi * 2 + x_lo), y: 4, z: 16, core: 2. Of those that a mesh axis runs over, the one named last changes fastest.
Arguments:
- img_queries: bfloat16 [2, 3072, 1216], P('cfg', 'seq')
- img_keys: bfloat16 [2, 3072, 1216], P('cfg', 'seq')
- img_values: bfloat16 [2, 3072, 1216], P('cfg', 'seq'), may hold values from -6 to 6
- text_keys: bfloat16 [2, 256, 1216], P('cfg', 'seq'), may hold values from -6 to 6
- text_values: bfloat16 [2, 256, 1216], P('cfg', 'seq'), may hold values from -18 to 18
- query_gain: float32 [64], replicated, may hold values from 0.5 to 8, as said below
- key_gain: float32 [64], replicated, may hold values from 0.5 to 8, as said below
- text_gain: float32 [64], replicated, may hold values from 0.5 to 8, as said below
- text_lengths: int32 [2], P('cfg'), may hold values from 1 to 256, as said below
- text_blocks: int32 [2, 256], P('cfg', 'seq'), may hold values from 0 to 1
- latent: float32 [3072, 64], P('seq', 'cfg'), may hold values from -6 to 6
- base_velocity: bfloat16 [2, 3072, 64], P('cfg', 'seq'), may hold values from -6 to 6
- out_weight: bfloat16 [1216, 64], replicated, may hold values from -1.25 to 1.25
- timestep: int32 [1], replicated, may hold values from 0 to 27
Outputs:
- next_latent: float32 [3072, 64], P('seq', 'cfg')
- denoised: float32 [3072, 64], P('seq', 'cfg')
Inputs may be any that keep to these rules, and one draw needn't show every extreme that they name: `query_gain`: gains are positive. `key_gain`: gains are positive. `text_gain`: gains are positive. `text_lengths`: one of the two halves has all 256 slots within its length.
All inputs are finite; a program needn't handle non-finite values.
Results may differ from a plain program's by a relative error of at most 0.007.
The roundings to bfloat16 on the way count: a program that leaves them out, or rounds other values in their place, can miss the bound.
Values may be sent and summed in bfloat16 or wider, within the bound.
No kernel may reach another device: no remote copies, remote signals or barrier semaphores. Data moves between devices by JAX's collectives and lax.ppermute only.
A program may use at most 128 MiB of HBM per device.

v0:
```python
import math

import jax
import jax.numpy as jnp
from jax import lax
from jax.sharding import PartitionSpec as P

STEPS = 28


epsilon = 1e-06
guidance = 3.5
shift_factor = 3.0
masked_score = -1e30


def from_partner(block, axis, stride):
    count = lax.axis_size(axis)
    route = []
    for low in range(count):
        high = low | 1 << stride
        if high != low and high < count:
            route += [(low, high), (high, low)]
    return lax.ppermute(block, axis, route)


def head_norm(values, gain_row):
    widened = values.astype(jnp.float32).reshape(values.shape[0], -1, gain_row.shape[0])
    scaled = (
        widened
        * lax.rsqrt(jnp.mean(widened * widened, axis=-1, keepdims=True) + epsilon)
        * gain_row
    )
    return scaled.astype(jnp.bfloat16)


def sigma_at(position):
    time_left = 1.0 - position / STEPS
    return shift_factor * time_left / (1.0 + (shift_factor - 1.0) * time_left)


def attend_block(running, queries, keys_block, values_block, usable):
    run_max, run_total, run_sum = running
    head_count = queries.shape[1]
    head_size = queries.shape[2]
    keys_heads = keys_block.reshape(keys_block.shape[0], head_count, head_size)
    values_heads = values_block.reshape(values_block.shape[0], head_count, head_size)
    scores = jnp.einsum("rhd,khd->hrk", queries, keys_heads, preferred_element_type=jnp.float32) * (
        1.0 / math.sqrt(head_size)
    )
    scores = jnp.where(usable[None, None, :], scores, masked_score)
    new_max = jnp.maximum(run_max, jnp.max(scores, axis=-1))
    factor = jnp.exp(run_max - new_max)
    weights_block = jnp.where(usable[None, None, :], jnp.exp(scores - new_max[..., None]), 0.0)
    run_total = run_total * factor + jnp.sum(weights_block, axis=-1)
    run_sum = run_sum * factor[..., None] + jnp.einsum(
        "hrk,khd->hrd",
        weights_block.astype(jnp.bfloat16),
        values_heads,
        preferred_element_type=jnp.float32,
    )
    return (new_max, run_total, run_sum)


def attend_text(running, queries, keys_block, values_block, usable_flags):
    usable = usable_flags == 1

    def take_block(state_in):
        return attend_block(state_in, queries, keys_block, values_block, usable)

    def keep_state(state_in):
        return state_in

    return lax.cond(jnp.any(usable), take_block, keep_state, running)


def on_device(
    img_queries,
    img_keys,
    img_values,
    text_keys,
    text_values,
    query_gain,
    key_gain,
    text_gain,
    text_lengths,
    text_blocks,
    latent,
    base_velocity,
    out_weight,
    timestep,
):
    head_size = query_gain.shape[0]
    head_count = img_queries.shape[2] // head_size
    row_count = img_queries.shape[1]
    text_count = text_keys.shape[1]
    queries = head_norm(img_queries[0], query_gain)
    keys_local = head_norm(img_keys[0], key_gain).reshape(row_count, head_count * head_size)
    values_local = img_values[0]
    text_keys_local = head_norm(text_keys[0], text_gain).reshape(text_count, head_count * head_size)
    text_values_local = text_values[0]
    slot_index = lax.axis_index("seq") * text_count + jnp.arange(text_count, dtype=jnp.int32)
    usable_text = ((slot_index < text_lengths[0]) & (text_blocks[0, 0] == 1)).astype(jnp.int32)
    initial = (
        jnp.full((head_count, row_count), masked_score, jnp.float32),
        jnp.zeros((head_count, row_count), jnp.float32),
        jnp.zeros((head_count, row_count, head_size), jnp.float32),
    )
    running = initial
    key_piece = lax.all_gather(keys_local, "seq", axis=0, tiled=True)
    value_piece = lax.all_gather(values_local, "seq", axis=0, tiled=True)
    text_key_piece = lax.all_gather(text_keys_local, "seq", axis=0, tiled=True)
    text_value_piece = lax.all_gather(text_values_local, "seq", axis=0, tiled=True)
    usable_piece = lax.all_gather(usable_text, "seq", axis=0, tiled=True)
    every_key = jnp.ones((key_piece.shape[0],), dtype=jnp.bool_)
    running = attend_block(running, queries, key_piece, value_piece, every_key)
    final_state = attend_text(running, queries, text_key_piece, text_value_piece, usable_piece)
    run_max, run_total, run_sum = final_state
    attended = (
        (run_sum / run_total[..., None])
        .transpose(1, 0, 2)
        .reshape(row_count, head_count * head_size)
        .astype(jnp.bfloat16)
    )
    velocity = base_velocity[0].astype(jnp.float32) + jnp.dot(
        attended, out_weight, preferred_element_type=jnp.float32
    )
    guide_half = lax.axis_index("cfg")
    half_width = latent.shape[1]
    own_part = lax.dynamic_slice_in_dim(velocity, guide_half * half_width, half_width, 1)
    sent_part = lax.dynamic_slice_in_dim(velocity, (1 - guide_half) * half_width, half_width, 1)
    partner = from_partner(sent_part, "cfg", 0)
    cond_part = jnp.where(guide_half == 0, own_part, partner)
    uncond_part = jnp.where(guide_half == 0, partner, own_part)
    guided = uncond_part + guidance * (cond_part - uncond_part)
    step_now = timestep[0].astype(jnp.float32)
    sigma_now = sigma_at(step_now)
    sigma_next = sigma_at(step_now + 1.0)
    next_latent = latent + (sigma_next - sigma_now) * guided
    denoised = latent - sigma_now * guided
    return (next_latent, denoised)


def solution(mesh):
    return jax.shard_map(
        on_device,
        mesh=mesh,
        in_specs=(
            P("cfg", "seq", None),
            P("cfg", "seq", None),
            P("cfg", "seq", None),
            P("cfg", "seq", None),
            P("cfg", "seq", None),
            P(),
            P(),
            P(),
            P("cfg"),
            P("cfg", "seq"),
            P("seq", "cfg"),
            P("cfg", "seq", None),
            P(),
            P(),
        ),
        out_specs=(P("seq", "cfg"), P("seq", "cfg")),
        check_vma=False,
    )
```

profile of v0, /device:TPU:1, one launch (start us, length us, event | category | flops | bytes accessed | tf_op | source)
XLA Modules:
  0.0 1482.1 jit_solution(14273524936408419100)
XLA Ops:
  7.2 0.0 copy-start
  7.2 0.0 copy-start.2
  7.2 0.0 all-gather.9.cloned.1.call-start
  7.2 0.8 convert_multiply_fusion
  8.0 0.1 mul.193
  8.1 0.1 reduce_sum.46
  8.2 0.1 mul.194
  8.3 0.1 mul.195
  8.4 0.0 copy-start.4
  8.5 0.7 mul.197
  9.1 0.1 mul.198
  9.2 1.4 fusion.27
  10.6 0.0 all-gather.9.cloned.1.call-update
  10.6 0.0 all-gather.7.cloned.1.call-start
  10.7 1.4 copy.44
  12.1 0.0 all-gather.7.cloned.1.call-update
  13.4 1.3 dynamic-slice
  14.7 0.7 fusion.33
  15.5 655.9 %all-reduce = s32[256]{0:T(256)S(1)} all-reduce(s32[256]{0:T(256)S(1)} %fusion.33), channel_id=1, replica_groups=mesh['cfg'=2,'seq'=256] {'seq'}, use_global_device_ids=true, to_apply=%add | all-reduce | flops 256 | bytes 2048
  671.3 0.6 fusion.35
  672.6 0.9 reshape.183
  673.5 0.7 mul.209
  674.1 0.1 mul.210
  674.2 0.7 fusion.31
  674.9 0.1 mul.205
  675.0 0.1 reduce_sum.48
  675.1 0.1 mul.206
  675.2 0.1 mul.207
  675.3 0.7 fusion.30
  676.0 358.8 %all-gather.3 = bf16[256,1,1216]{2,1,0:T(2,128)(2,1)S(1)} all-gather(bf16[1,1,1216]{2,1,0:T(2,128)(2,1)S(1)} %fusion.30), channel_id=1, replica_groups=mesh['cfg'=2,'seq'=256] {'seq'}, dimensions={0}, use_global_device_ids=true | all-gather | bytes 625024 | tf_op jit(solution)/shard_map/all_gather | solution.py:112
  1034.8 1.3 copy.46
  1036.0 0.0 copy-done.2
  1036.1 353.9 %all-gather.1 = bf16[256,1,1216]{2,1,0:T(2,128)(2,1)S(1)} all-gather(bf16[1,1,1216]{2,1,0:T(2,128)(2,1)S(1)} %copy-done.2), channel_id=3, replica_groups=mesh['cfg'=2,'seq'=256] {'seq'}, dimensions={0}, use_global_device_ids=true | all-gather | bytes 625024 | tf_op jit(solution)/shard_map/all_gather | solution.py:113
  1389.9 1.3 copy.47
  1391.2 0.1 multiply_reduce_fusion
  1391.3 0.0 copy-done.4
  1391.3 0.1 multiply_convert_fusion
  1391.5 0.0 all-gather.9.cloned.1.call-done
  1391.5 24.8 %reshape.174 = bf16[3072,19,64]{2,1,0:T(8,128)(2,1)} reshape(bf16[256,12,1216]{2,1,0:T(8,128)(2,1)} %all-gather.9.cloned.1.call-done) | data formatting | bytes 14942208 | tf_op jit(solution)/shard_map/reshape | solution.py:46
  1416.3 12.3 fusion.37
  1428.5 2.7 fusion.15
  1431.3 0.0 all-gather.7.cloned.1.call-done
  1431.3 31.0 %copy.45 = bf16[1,3072,1216]{1,2,0:T(8,128)(2,1)} copy(bf16[1,3072,1216]{2,0,1:T(2,128)(2,1)} %all-gather.7.cloned.1.call-done) | data formatting | bytes 14942208 | tf_op jit(solution)/shard_map/all_gather | solution.py:111
  1462.3 0.0 copy-start.3
  1462.3 0.0 copy-start.1
  1462.3 6.4 fusion.19
  1468.7 0.9 conditional.1
  1468.8 0.3 fusion.36
  1469.1 0.2 fusion.2
  1469.3 0.3 convolution_add_fusion
  1469.6 0.1 fusion.26
  1469.8 0.1 convert_element_type.127
  1469.9 0.0 copy-done
  1469.9 0.0 copy-done.3
  1469.9 0.2 convolution_add_fusion.1
  1470.1 0.1 constant_dynamic-slice_fusion
  1470.2 2.2 collective-permute-start
  1473.2 1.4 collective-permute-done
  1474.6 0.0 copy-done.1
  1474.6 0.7 multiply_subtract_fusion
  (9 shorter events, 0.1 us)
Async XLA Ops:
  7.2 1462.7 %copy-start = (bf16[1216,64]{0,1:T(8,128)(2,1)S(1)}, bf16[1216,64]{0,1:T(8,128)(2,1)}, u32[]{:S(2)}) copy-start(bf16[1216,64]{0,1:T(8,128)(2,1)} %param.28) | copy-start | bytes 466948
  7.2 1028.9 %copy-start.2 = (bf16[1,1,1216]{2,1,0:T(2,128)(2,1)S(1)}, bf16[1,1,1216]{2,1,0:T(2,128)(2,1)}, u32[]{:S(2)}) copy-start(bf16[1,1,1216]{2,1,0:T(2,128)(2,1)} %param.20) | copy-start | bytes 7300
  7.2 1384.3 %all-gather.9.cloned.1.call-start = ((), (), s32[]{:S(2)}) async-start(), calls=%async_computation.1 | async-start | bytes 10526720 | tf_op jit(solution)/shard_map/all_gather | solution.py:110
  8.4 1382.9 %copy-start.4 = (f32[64]{0:T(128)S(1)}, f32[64]{0:T(128)}, u32[]{:S(2)}) copy-start(f32[64]{0:T(128)} %param.21) | copy-start | bytes 772
  10.6 1420.7 %all-gather.7.cloned.1.call-start = ((), (), s32[]{:S(2)}) async-start(), calls=%async_computation | async-start | bytes 15790080 | tf_op jit(solution)/shard_map/all_gather | solution.py:111
  1462.3 7.6 copy-start.3
  1462.3 12.2 copy-start.1
  1470.2 4.4 collective-permute-start
Sparse Core Ops, SparseCore 0:
  12.5 234.6 all-gather.8
  252.0 238.5 all-gather.6
where the time goes:
time: 1480 us
  blocking collectives  1370 us (93%)
  local copies, waits for them, and re-layouts  64.1 us (4%)
  matrix products  19.4 us (1%)
  between operations  16.9 us (1%)
    unnamed x1, blocking collectives  656 us
    all_gather x1, blocking collectives, on_device(): text_key_piece = lax.all_gather(text_keys_local, 'seq', axis=0, tiled=True)  359 us
    all_gather x1, blocking collectives, on_device(): lax.all_gather(text_values_local, 'seq', axis=0, tiled=True)  354 us
    all_gather x1, local copies, waits for them, and re-layouts, on_device(): value_piece = lax.all_gather(values_local, 'seq', axis=0, tiled=True)  31 us
  transfers between devices with their start and end apart: 3, of which 1 were waited for; matrix products, arithmetic and copies ran while one was open for 3% of the time, Pallas kernels for 0%

commit v1 on v0

v1 whole, which is shorter than its diff:
```python
import jax
import jax.numpy as jnp
from jax import lax
from jax.experimental import pallas as pl
from jax.experimental.pallas import tpu as pltpu
from jax.sharding import Mesh, PartitionSpec as P

STEPS = 28
HEADS = 19
DH = 64
GROUPS = 4
PER = 5
HALF = 6

epsilon = 1e-06
guidance = 3.5
shift_factor = 3.0
masked_score = -1e30

G = ("zl", "core")
R = ("zh",)
C = ("y", "xh")
SEQ = ("y", "xh", "zh", "zl", "core")

f32 = jnp.float32
bf16 = jnp.bfloat16


def sigma_at(position):
    time_left = 1.0 - position / STEPS
    return shift_factor * time_left / (1.0 + (shift_factor - 1.0) * time_left)


def left_lanes(shape):
    return lax.broadcasted_iota(jnp.int32, shape, len(shape) - 1) < DH


def swap(x):
    return pltpu.roll(x, DH, x.ndim - 1)


def normed(x, gain):
    left = left_lanes(x.shape)
    squares = x * x
    sum_left = jnp.sum(jnp.where(left, squares, 0.0), axis=-1, keepdims=True)
    sum_right = jnp.sum(jnp.where(left, 0.0, squares), axis=-1, keepdims=True)
    root = jnp.where(
        left,
        lax.rsqrt(sum_left / DH + epsilon),
        lax.rsqrt(sum_right / DH + epsilon),
    )
    return (x * root * gain).astype(bf16).astype(f32)


def fold(tile, odd):
    low, high = tile[:HALF], tile[HALF:]
    left = left_lanes(low.shape)
    if odd:
        return jnp.where(left, swap(low), high)
    return jnp.where(left, low, swap(high))


def pack_kernel(copies_q, copies_kv, q, k, v, tk, tv, gains, flag, q_out, kv_out):
    query_gain = gains[0:1]
    key_gain = gains[1:2]
    text_gain = gains[2:3]
    usable = flag[0, 0].astype(f32)
    pairs = (HEADS + 1) // 2
    zero2 = jnp.zeros((2, 128), f32)
    zero1 = jnp.zeros((1, 128), f32)
    left1 = left_lanes((1, 128))
    heads = []
    for p in range(pairs):
        wide = 128 if 128 * (p + 1) <= HEADS * DH else DH
        lanes = slice(128 * p, 128 * p + wide)

        def load(ref):
            x = ref[:, lanes].astype(f32)
            if wide < 128:
                x = jnp.concatenate([x, jnp.zeros((x.shape[0], 128 - wide), f32)], axis=1)
            return x

        qt = normed(load(q), query_gain) * 0.125
        kt = normed(load(k), key_gain)
        vt = load(v)
        tkt = normed(load(tk), text_gain)
        tvt = load(tv)
        for odd in range(2):
            q6 = fold(qt, odd)
            k6 = fold(kt, odd)
            v6 = fold(vt, odd)
            tk1 = swap(tkt) if odd else tkt
            tv1 = swap(tvt) if odd else tvt
            tk1 = jnp.where(left1, tk1, usable)
            tv1 = jnp.where(left1, tv1, 0.0)
            heads.append(
                (
                    jnp.concatenate([q6, zero2], axis=0),
                    jnp.concatenate([k6, tk1, zero1, v6, tv1, zero1], axis=0),
                )
            )
    for g in range(GROUPS):
        own = heads[PER * g : PER * (g + 1)]
        q_msg = jnp.concatenate([h[0] for h in own], axis=0).astype(bf16)
        kv_msg = jnp.concatenate([h[1] for h in own], axis=0).astype(bf16)
        for c in range(copies_q):
            q_out[g * copies_q + c] = q_msg
        for c in range(copies_kv):
            kv_out[g * copies_kv + c] = kv_msg


def rows_of(block):
    return block.reshape(block.shape[0] * block.shape[1], block.shape[2])


def dot_t(a, b):
    return lax.dot_general(a, b, (((1,), (1,)), ((), ())), preferred_element_type=f32)


def attend_kernel(q_in, kv_in, out):
    peers_q = q_in.shape[0]
    peers_k = kv_in.shape[0]
    keys = peers_k * 8
    queries = peers_q * 8
    left_k = left_lanes((keys, 128))
    left_q = left_lanes((queries, 128))
    lane_q = lax.broadcasted_iota(jnp.int32, (queries, 128), 1)
    row_kind = lax.broadcasted_iota(jnp.int32, (1, keys), 1) & 7
    image = row_kind < HALF
    stats = jnp.zeros((queries, 128), f32)
    tiles = []
    for j in range(PER):
        q = rows_of(q_in[:, 8 * j : 8 * j + 8, :].astype(f32))
        kv = kv_in[:, 16 * j : 16 * j + 16, :].astype(f32)
        k = rows_of(kv[:, 0:8])
        v = rows_of(kv[:, 8:16])
        if j == 0:
            pick = (lax.broadcasted_iota(jnp.int32, (8, 128), 1) == DH).astype(bf16)
            flags = dot_t(pick, k.astype(bf16))[0:1]
            text = (row_kind == HALF) & (flags > 0.5)
            bias_l = jnp.where(image | text, 0.0, masked_score)
            bias_r = jnp.where(image, 0.0, masked_score)
        q_same = q.astype(bf16)
        q_swap = swap(q).astype(bf16)
        k_l = jnp.where(left_k, k, 0.0).astype(bf16)
        k_r = jnp.where(left_k, 0.0, k).astype(bf16)
        v_same = v.astype(bf16)
        v_swap = swap(v).astype(bf16)
        sides = []
        for side in range(2):
            s_l = dot_t(q_swap if side else q_same, k_l) + bias_l
            s_r = dot_t(q_same if side else q_swap, k_r) + bias_r
            top = jnp.max(jnp.maximum(s_l, s_r), axis=-1, keepdims=True)
            top = top.astype(bf16).astype(f32)
            p_l = jnp.exp(s_l - top)
            p_r = jnp.exp(s_r - top)
            den = jnp.sum(p_l + p_r, axis=-1, keepdims=True)
            num = jnp.dot(
                p_l.astype(bf16), v_swap if side else v_same, preferred_element_type=f32
            ) + jnp.dot(
                p_r.astype(bf16), v_same if side else v_swap, preferred_element_type=f32
            )
            den_hi = den.astype(bf16).astype(f32)
            lane = 8 * side + j
            stats = jnp.where(lane_q == lane, top, stats)
            stats = jnp.where(lane_q == lane + 16, den_hi, stats)
            stats = jnp.where(lane_q == lane + 32, den - den_hi, stats)
            sides.append(num)
        tiles.append(jnp.where(left_q, sides[0], sides[1]).reshape(peers_q, 8, 128))
    tiles.append(stats.reshape(peers_q, 8, 128))
    for j in range(0, PER + 1, 2):
        pair = jnp.concatenate([tiles[j], tiles[j + 1]], axis=1)
        out[:, 8 * j : 8 * j + 16, :] = pair.astype(bf16)


def merge_kernel(parts_in, weight, out):
    blocks = parts_in.shape[0] // GROUPS
    left = left_lanes((blocks, 8, 128))
    left8 = left_lanes((8, 128))
    total = jnp.zeros((16, DH), f32)
    for g in range(GROUPS):
        part = parts_in[g * blocks : (g + 1) * blocks].astype(f32)
        stats = part[:, 8 * PER :, :]
        den = pltpu.roll(stats, 128 - 16, 2) + pltpu.roll(stats, 128 - 32, 2)
        top = jnp.max(stats, axis=0, keepdims=True)
        scale = jnp.exp(stats - top)
        whole = jnp.sum(scale * den, axis=0, keepdims=True)
        share = scale / whole
        for j in range(PER):
            h = PER * g + j
            if h >= HEADS:
                continue
            each = jnp.where(left, share[:, :, j : j + 1], share[:, :, 8 + j : 9 + j])
            attended = jnp.sum(each * part[:, 8 * j : 8 * j + 8, :], axis=0)
            attended = attended.astype(bf16).astype(f32)
            both = jnp.concatenate(
                [jnp.where(left8, attended, 0.0), jnp.where(left8, 0.0, attended)], axis=0
            ).astype(bf16)
            rows = weight[DH * h : DH * (h + 1), :]
            total += jnp.dot(
                both, jnp.concatenate([rows, rows], axis=0), preferred_element_type=f32
            )
    out[...] = total


def on_device(
    img_queries,
    img_keys,
    img_values,
    text_keys,
    text_values,
    query_gain,
    key_gain,
    text_gain,
    text_lengths,
    text_blocks,
    latent,
    base_velocity,
    out_weight,
    timestep,
):
    count_c = lax.axis_size(C)
    count_r = lax.axis_size(R)
    slot = lax.axis_index(SEQ)
    usable = ((slot < text_lengths[0]) & (text_blocks[0, 0] == 1)).astype(jnp.int32)
    gains = jnp.stack([query_gain, key_gain, text_gain])
    gains = jnp.concatenate([gains, gains], axis=1)
    q_msg, kv_msg = pl.pallas_call(
        lambda *refs: pack_kernel(count_c, count_r, *refs),
        out_shape=(
            jax.ShapeDtypeStruct((GROUPS * count_c, 8 * PER, 128), bf16),
            jax.ShapeDtypeStruct((GROUPS * count_r, 16 * PER, 128), bf16),
        ),
        in_specs=[pl.BlockSpec(memory_space=pltpu.VMEM)] * 6
        + [pl.BlockSpec(memory_space=pltpu.SMEM)],
        name="pack",
    )(
        img_queries[0],
        img_keys[0],
        img_values[0],
        text_keys[0],
        text_values[0],
        gains,
        usable.reshape(1, 1),
    )
    q_got = lax.all_to_all(q_msg, G + C, 0, 0, tiled=True)
    kv_got = lax.all_to_all(kv_msg, G + R, 0, 0, tiled=True)
    parts = pl.pallas_call(
        attend_kernel,
        out_shape=jax.ShapeDtypeStruct((GROUPS * count_c, 8 * PER + 8, 128), bf16),
        name="attend",
    )(q_got, kv_got)
    parts_got = lax.all_to_all(parts, G + C, 0, 0, tiled=True)
    change = pl.pallas_call(
        merge_kernel, out_shape=jax.ShapeDtypeStruct((16, DH), f32), name="merge"
    )(parts_got, out_weight)
    change = jnp.concatenate([change[:HALF], change[8 : 8 + HALF]], axis=0)
    velocity = base_velocity[0].astype(f32) + change
    guide_half = lax.axis_index("cfg")
    width = latent.shape[1]
    own_part = jnp.where(guide_half == 0, velocity[:, :width], velocity[:, width:])
    sent_part = jnp.where(guide_half == 0, velocity[:, width:], velocity[:, :width])
    partner = lax.ppermute(sent_part, "cfg", [(0, 1), (1, 0)])
    cond_part = jnp.where(guide_half == 0, own_part, partner)
    uncond_part = jnp.where(guide_half == 0, partner, own_part)
    guided = uncond_part + guidance * (cond_part - uncond_part)
    step_now = timestep[0].astype(f32)
    sigma_now = sigma_at(step_now)
    sigma_next = sigma_at(step_now + 1.0)
    next_latent = latent + (sigma_next - sigma_now) * guided
    denoised = latent - sigma_now * guided
    return (next_latent, denoised)


def build(fine):
    return jax.shard_map(
        on_device,
        mesh=fine,
        in_specs=(
            P("cfg", SEQ, None),
            P("cfg", SEQ, None),
            P("cfg", SEQ, None),
            P("cfg", SEQ, None),
            P("cfg", SEQ, None),
            P(),
            P(),
            P(),
            P("cfg"),
            P("cfg", SEQ),
            P(SEQ, "cfg"),
            P("cfg", SEQ, None),
            P(),
            P(),
        ),
        out_specs=(P(SEQ, "cfg"), P(SEQ, "cfg")),
        check_vma=False,
    )


def solution(mesh):
    devices = mesh.devices.reshape(2, 4, 2, 8, 2, 2)
    return build(Mesh(devices, ("cfg",) + SEQ))
```

time: 1480 us -> 109 us (0.07)
  the two profiles are of different devices: /device:TPU:1 before, /device:TPU:64 now
where the time goes in v1:
time: 109 us; the launch traced here: 108 us
  blocking collectives  70.6 us (65%)
  waiting for transfers between devices  12.5 us (11%)
  Pallas kernels  10.6 us (10%)
  starting transfers between devices  6.51 us (6%)
  local copies, waits for them, and re-layouts  3.05 us (3%)
  between operations  2.75 us (3%)
  other arithmetic  2.02 us (2%)
    all_to_all x1, blocking collectives, on_device(): kv_got = lax.all_to_all(kv_msg, G + R, 0, 0, tiled=True)  51.1 us
    all_to_all x1, blocking collectives, on_device(): q_got = lax.all_to_all(q_msg, G + C, 0, 0, tiled=True)  19.4 us
    all_to_all x1, waiting for transfers between devices, on_device(): parts_got = lax.all_to_all(parts, G + C, 0, 0, tiled=True)  10.2 us
    pallas_call x1, Pallas kernels, on_device(): pl.pallas_call(attend_kernel, out_shape=jax.ShapeDtypeStruct((GROUPS * co...  5.45 us
    all_to_all x1, starting transfers between devices, on_device(): parts_got = lax.all_to_all(parts, G + C, 0, 0, tiled=True)  4.01 us
    pallas_call x1, Pallas kernels, on_device(): pl.pallas_call(lambda *refs: pack_kernel(count_c, count_r, *refs), out_sh...  2.59 us
    pallas_call x1, Pallas kernels, on_device(): pl.pallas_call(merge_kernel, out_shape=jax.ShapeDtypeStruct((16, DH), f32...  2.59 us
    ppermute x1, starting transfers between devices, on_device(): partner = lax.ppermute(sent_part, 'cfg', [(0, 1), (1, 0)])  2.5 us
  transfers between devices with their start and end apart: 2, of which 2 were waited for; matrix products, arithmetic and copies ran while one was open for 1% of the time, Pallas kernels for 0%

profile of v1, /device:TPU:64, one launch (start us, length us, event | category | flops | bytes accessed | tf_op | source)
XLA Modules:
  0.0 108.0 jit_solution(617479740151194163)
XLA Ops:
  1.9 0.0 copy-start.5
  1.9 0.0 copy-start.6
  2.0 0.0 copy-start.7
  2.0 0.6 copy-done.5
  2.6 0.0 copy-done.6
  2.6 0.0 copy-done.7
  2.6 0.7 maximum_maximum_fusion.refs_5_
  3.3 2.6 %pack.1 = (bf16[32,40,128]{2,1,0:T(8,128)(2,1)}, bf16[32,80,128]{2,1,0:T(8,128)(2,1)}) custom-call(bf16[12,1216]{1,0:T(8,128)(2,1)} %bitcast.17, bf16[12,1216]{1,0:T(8,128)(2,1)} %bitcast.18, bf16[12,1216]{1,0:T(8,128)(2,1)} %bitcast.19, bf16[1,1216]{1,0:T(2,128)(2,1)} %bitcast.20, bf16[1,1216]{1,0:T(2,128)(2,1)} %bitcast.21, ...), custom_call_target="tpu_custom_call" | custom-call | tf_op jit(solution)/shard_map/pack/pallas_call | solution.py:228
  5.9 0.0 copy-start.1
  5.9 19.4 %all_to_all.15.q_in = bf16[32,40,128]{2,1,0:T(8,128)(2,1)} all-to-all(bf16[32,40,128]{2,1,0:T(8,128)(2,1)} %get-tuple-element.4), channel_id=1, replica_groups=mesh['cfg'=2,'y'=4,'xh'=2,'zh'=8,'zl'=2,'core'=2] {'zl','core','y','xh'}, dimensions={0} | all-to-all | bytes 655360 | tf_op jit(solution)/shard_map/all_to_all | solution.py:246
  25.3 0.0 copy-done.1
  25.3 51.1 %all_to_all.16.kv_in = bf16[32,80,128]{2,1,0:T(8,128)(2,1)} all-to-all(bf16[32,80,128]{2,1,0:T(8,128)(2,1)S(1)} %copy-done.1), channel_id=1, replica_groups=mesh['cfg'=2,'y'=4,'xh'=2,'zh'=8,'zl'=2,'core'=2] {'zl','core','zh'}, dimensions={0} | all-to-all | bytes 1310720 | tf_op jit(solution)/shard_map/all_to_all | solution.py:247
  76.4 5.4 %attend.1 = bf16[32,48,128]{2,1,0:T(8,128)(2,1)} custom-call(bf16[32,40,128]{2,1,0:T(8,128)(2,1)} %all_to_all.15.q_in, bf16[32,80,128]{2,1,0:T(8,128)(2,1)} %all_to_all.16.kv_in), custom_call_target="tpu_custom_call" | custom-call | tf_op jit(solution)/shard_map/attend/pallas_call | solution.py:248
  81.9 0.0 copy-start.2
  81.9 4.0 %all-to-all-start.2 = ((bf16[32,48,128]{2,1,0:T(8,128)(2,1)}), bf16[32,48,128]{2,1,0:T(8,128)(2,1)S(1)}, u32[]{:S(2)}, u32[]{:S(2)}) async-start(bf16[32,48,128]{2,1,0:T(8,128)(2,1)} %attend.1), calls=%async_computation.2 | async-start | bytes 786432 | tf_op jit(solution)/shard_map/all_to_all | solution.py:253
  85.9 0.0 copy-done.2
  85.9 0.9 copy.16.weight
  86.8 10.2 %all-to-all-done.2.parts_in = bf16[32,48,128]{2,1,0:T(8,128)(2,1)S(1)} async-done(((bf16[32,48,128]{2,1,0:T(8,128)(2,1)}), bf16[32,48,128]{2,1,0:T(8,128)(2,1)S(1)}, u32[]{:S(2)}, u32[]{:S(2)}) %all-to-all-start.2) | async-done | bytes 393248 | tf_op jit(solution)/shard_map/all_to_all | solution.py:253
  97.1 0.0 copy-start
  97.1 0.7 copy-done
  97.8 2.6 %merge.1 = f32[16,64]{1,0:T(8,128)} custom-call(bf16[32,48,128]{2,1,0:T(8,128)(2,1)} %copy-done, bf16[1216,64]{1,0:T(8,128)(2,1)} %copy.16.weight), custom_call_target="tpu_custom_call" | custom-call | tf_op jit(solution)/shard_map/merge/pallas_call | solution.py:254
  100.4 0.0 copy-start.4
  100.4 0.7 fusion
  101.1 0.0 copy-done.4
  101.1 0.1 slice_select_fusion
  101.2 2.5 %collective-permute-start = (f32[12,32]{1,0:T(8,128)S(1)}, f32[12,32]{1,0:T(8,128)S(1)}, u32[]{:S(2)}, u32[]{:S(2)}) collective-permute-start(f32[12,32]{1,0:T(8,128)S(1)} %slice_select_fusion), channel_id=1, source_target_pairs={{0,256},{256,0},{1,257},{257,1},{2,258},{258,2},{3,259},{259,3},{4... | collective-permute-start | bytes 4616 | tf_op jit(solution)/shard_map/ppermute | solution.py:263
  104.4 0.0 copy-start.3
  104.5 2.3 %collective-permute-done = f32[12,32]{1,0:T(8,128)S(1)} collective-permute-done((f32[12,32]{1,0:T(8,128)S(1)}, f32[12,32]{1,0:T(8,128)S(1)}, u32[]{:S(2)}, u32[]{:S(2)}) %collective-permute-start) | collective-permute-done | bytes 1568 | tf_op jit(solution)/shard_map/ppermute | solution.py:263
  106.8 0.0 copy-done.3
  106.8 0.7 multiply_subtract_fusion
  107.4 0.6 multiply_add_fusion
  (1 shorter events, 0.0 us)
Async XLA Ops:
  1.9 0.7 copy-start.5
  1.9 0.7 copy-start.6
  2.0 0.7 copy-start.7
  5.9 19.4 %copy-start.1 = (bf16[32,80,128]{2,1,0:T(8,128)(2,1)S(1)}, bf16[32,80,128]{2,1,0:T(8,128)(2,1)}, u32[]{:S(2)}) copy-start(bf16[32,80,128]{2,1,0:T(8,128)(2,1)} %get-tuple-element.5) | copy-start | bytes 1966084
  81.9 4.0 %copy-start.2 = (bf16[1216,64]{0,1:T(8,128)(2,1)S(1)}, bf16[1216,64]{0,1:T(8,128)(2,1)}, u32[]{:S(2)}) copy-start(bf16[1216,64]{0,1:T(8,128)(2,1)} %param.26) | copy-start | bytes 466948
  81.9 15.2 %all-to-all-start.2 = ((bf16[32,48,128]{2,1,0:T(8,128)(2,1)}), bf16[32,48,128]{2,1,0:T(8,128)(2,1)S(1)}, u32[]{:S(2)}, u32[]{:S(2)}) async-start(bf16[32,48,128]{2,1,0:T(8,128)(2,1)} %attend.1), calls=%async_computation.2 | async-start | bytes 786432 | tf_op jit(solution)/shard_map/all_to_all | solution.py:253
  97.1 0.7 copy-start
  100.4 0.7 copy-start.4
  101.2 5.5 %collective-permute-start = (f32[12,32]{1,0:T(8,128)S(1)}, f32[12,32]{1,0:T(8,128)S(1)}, u32[]{:S(2)}, u32[]{:S(2)}) collective-permute-start(f32[12,32]{1,0:T(8,128)S(1)} %slice_select_fusion), channel_id=1, source_target_pairs={{0,256},{256,0},{1,257},{257,1},{2,258},{258,2},{3,259},{259,3},{4... | collective-permute-start | bytes 4616 | tf_op jit(solution)/shard_map/ppermute | solution.py:263
  104.4 2.4 %copy-start.3 = (f32[12,32]{1,0:T(8,128)S(1)}, f32[12,32]{1,0:T(8,128)}, u32[]{:S(2)}) copy-start(f32[12,32]{1,0:T(8,128)} %param.24) | copy-start | bytes 4612

commit v2 on v1

--- a/solution.py
+++ b/solution.py
@@ -4,6 +4,7 @@
 from jax.experimental import pallas as pl
 from jax.experimental.pallas import tpu as pltpu
 from jax.sharding import Mesh, PartitionSpec as P
+
 
 STEPS = 28
 HEADS = 19
@@ -60,53 +61,67 @@
     return jnp.where(left, low, swap(high))
 
 
-def pack_kernel(copies_q, copies_kv, q, k, v, tk, tv, gains, flag, q_out, kv_out):
-    query_gain = gains[0:1]
-    key_gain = gains[1:2]
-    text_gain = gains[2:3]
-    usable = flag[0, 0].astype(f32)
-    pairs = (HEADS + 1) // 2
-    zero2 = jnp.zeros((2, 128), f32)
-    zero1 = jnp.zeros((1, 128), f32)
-    left1 = left_lanes((1, 128))
-    heads = []
-    for p in range(pairs):
+def head_tiles(refs, gains, wanted):
+    for p in range((HEADS + 1) // 2):
         wide = 128 if 128 * (p + 1) <= HEADS * DH else DH
         lanes = slice(128 * p, 128 * p + wide)
-
-        def load(ref):
+        tiles = []
+        for ref, gain in zip(refs, gains):
             x = ref[:, lanes].astype(f32)
             if wide < 128:
                 x = jnp.concatenate([x, jnp.zeros((x.shape[0], 128 - wide), f32)], axis=1)
-            return x
-
-        qt = normed(load(q), query_gain) * 0.125
-        kt = normed(load(k), key_gain)
-        vt = load(v)
-        tkt = normed(load(tk), text_gain)
-        tvt = load(tv)
+            tiles.append(x if gain is None else normed(x, gain))
         for odd in range(2):
-            q6 = fold(qt, odd)
-            k6 = fold(kt, odd)
-            v6 = fold(vt, odd)
-            tk1 = swap(tkt) if odd else tkt
-            tv1 = swap(tvt) if odd else tvt
-            tk1 = jnp.where(left1, tk1, usable)
-            tv1 = jnp.where(left1, tv1, 0.0)
-            heads.append(
-                (
-                    jnp.concatenate([q6, zero2], axis=0),
-                    jnp.concatenate([k6, tk1, zero1, v6, tv1, zero1], axis=0),
-                )
-            )
+            wanted(tiles, odd)
+
+
+def send_copies(out, copies, heads):
     for g in range(GROUPS):
-        own = heads[PER * g : PER * (g + 1)]
-        q_msg = jnp.concatenate([h[0] for h in own], axis=0).astype(bf16)
-        kv_msg = jnp.concatenate([h[1] for h in own], axis=0).astype(bf16)
-        for c in range(copies_q):
-            q_out[g * copies_q + c] = q_msg
-        for c in range(copies_kv):
-            kv_out[g * copies_kv + c] = kv_msg
+        message = jnp.concatenate(heads[PER * g : PER * (g + 1)], axis=0).astype(bf16)
+        for c in range(copies):
+            out[g * copies + c] = message
+
+
+def pack_keys(copies, k, v, tk, tv, gains, flag, out):
+    usable = flag[0, 0].astype(f32)
+    zero = jnp.zeros((1, 128), f32)
+    left = left_lanes((1, 128))
+    heads = []
+
+    def add(tiles, odd):
+        kt, vt, tkt, tvt = tiles
+        tk1 = swap(tkt) if odd else tkt
+        tv1 = swap(tvt) if odd else tvt
+        tk1 = jnp.where(left, tk1, usable)
+        tv1 = jnp.where(left, tv1, 0.0)
+        rows = [fold(kt, odd), tk1, zero, fold(vt, odd), tv1, zero]
+        heads.append(jnp.concatenate(rows, axis=0))
+
+    head_tiles((k, v, tk, tv), (gains[0:1], None, gains[1:2], None), add)
+    send_copies(out, copies, heads)
+
+
+def pack_queries(place, q, gains, out):
+    zero = jnp.zeros((2, 128), f32)
+    heads = []
+
+    def add(tiles, odd):
+        heads.append(jnp.concatenate([fold(tiles[0], odd) * 0.125, zero], axis=0))
+
+    head_tiles((q,), (gains[...],), add)
+    for g in range(GROUPS):
+        message = jnp.concatenate(heads[PER * g : PER * (g + 1)], axis=0).astype(bf16)
+        out[jnp.bitwise_xor(place[0], g)] = message
+
+
+def spread_kernel(*refs):
+    *blocks, same, other = refs
+    rows = 8 * GROUPS
+    for d, block in enumerate(blocks):
+        for j in range(PER):
+            q = rows_of(block[:, 8 * j : 8 * j + 8, :].astype(f32))
+            same[j, rows * d : rows * (d + 1), :] = q.astype(bf16)
+            other[j, rows * d : rows * (d + 1), :] = swap(q).astype(bf16)
 
 
 def rows_of(block):
@@ -117,8 +132,8 @@
     return lax.dot_general(a, b, (((1,), (1,)), ((), ())), preferred_element_type=f32)
 
 
-def attend_kernel(q_in, kv_in, out):
-    peers_q = q_in.shape[0]
+def attend_kernel(place, same, other, kv_in, out):
+    peers_q = same.shape[1] // 8
     peers_k = kv_in.shape[0]
     keys = peers_k * 8
     queries = peers_q * 8
@@ -130,7 +145,6 @@
     stats = jnp.zeros((queries, 128), f32)
     tiles = []
     for j in range(PER):
-        q = rows_of(q_in[:, 8 * j : 8 * j + 8, :].astype(f32))
         kv = kv_in[:, 16 * j : 16 * j + 16, :].astype(f32)
         k = rows_of(kv[:, 0:8])
         v = rows_of(kv[:, 8:16])
@@ -140,8 +154,8 @@
             text = (row_kind == HALF) & (flags > 0.5)
             bias_l = jnp.where(image | text, 0.0, masked_score)
             bias_r = jnp.where(image, 0.0, masked_score)
-        q_same = q.astype(bf16)
-        q_swap = swap(q).astype(bf16)
+        q_same = same[j]
+        q_swap = other[j]
         k_l = jnp.where(left_k, k, 0.0).astype(bf16)
         k_r = jnp.where(left_k, 0.0, k).astype(bf16)
         v_same = v.astype(bf16)
@@ -169,8 +183,11 @@
         tiles.append(jnp.where(left_q, sides[0], sides[1]).reshape(peers_q, 8, 128))
     tiles.append(stats.reshape(peers_q, 8, 128))
     for j in range(0, PER + 1, 2):
-        pair = jnp.concatenate([tiles[j], tiles[j + 1]], axis=1)
-        out[:, 8 * j : 8 * j + 16, :] = pair.astype(bf16)
+        pair = jnp.concatenate([tiles[j], tiles[j + 1]], axis=1).astype(bf16)
+        for b in range(peers_q):
+            owner = jnp.bitwise_xor(place[0], b % GROUPS) * (peers_q // GROUPS)
+            owner += jnp.bitwise_xor(place[1], b // GROUPS)
+            out[owner, 8 * j : 8 * j + 16, :] = pair[b]
 
 
 def merge_kernel(parts_in, weight, out):
@@ -223,33 +240,45 @@
     count_r = lax.axis_size(R)
     slot = lax.axis_index(SEQ)
     usable = ((slot < text_lengths[0]) & (text_blocks[0, 0] == 1)).astype(jnp.int32)
-    gains = jnp.stack([query_gain, key_gain, text_gain])
-    gains = jnp.concatenate([gains, gains], axis=1)
-    q_msg, kv_msg = pl.pallas_call(
-        lambda *refs: pack_kernel(count_c, count_r, *refs),
-        out_shape=(
-            jax.ShapeDtypeStruct((GROUPS * count_c, 8 * PER, 128), bf16),
-            jax.ShapeDtypeStruct((GROUPS * count_r, 16 * PER, 128), bf16),
-        ),
-        in_specs=[pl.BlockSpec(memory_space=pltpu.VMEM)] * 6
-        + [pl.BlockSpec(memory_space=pltpu.SMEM)],
-        name="pack",
-    )(
-        img_queries[0],
-        img_keys[0],
-        img_values[0],
-        text_keys[0],
-        text_values[0],
-        gains,
-        usable.reshape(1, 1),
-    )
-    q_got = lax.all_to_all(q_msg, G + C, 0, 0, tiled=True)
+    vmem = pl.BlockSpec(memory_space=pltpu.VMEM)
+    smem = pl.BlockSpec(memory_space=pltpu.SMEM)
+    twice = jnp.concatenate([jnp.stack([key_gain, text_gain])] * 2, axis=1)
+    query_twice = jnp.concatenate([query_gain, query_gain]).reshape(1, 2 * DH)
+    peers_q = GROUPS * count_c
+    place = jnp.stack([lax.axis_index(G), lax.axis_index(C)])
+    kv_msg = pl.pallas_call(
+        lambda *refs: pack_keys(count_r, *refs),
+        out_shape=jax.ShapeDtypeStruct((GROUPS * count_r, 16 * PER, 128), bf16),
+        in_specs=[vmem] * 5 + [smem],
+        name="pack_keys",
+    )(img_keys[0], img_values[0], text_keys[0], text_values[0], twice, usable.reshape(1, 1))
     kv_got = lax.all_to_all(kv_msg, G + R, 0, 0, tiled=True)
+    q_msg = pl.pallas_call(
+        pack_queries,
+        out_shape=jax.ShapeDtypeStruct((GROUPS, 8 * PER, 128), bf16),
+        in_specs=[smem, vmem, vmem],
+        name="pack_queries",
+    )(place, img_queries[0], query_twice)
+    got = [q_msg[:1]]
+    for d in range(1, GROUPS):
+        route = [(i, i ^ d) for i in range(GROUPS)]
+        got.append(lax.ppermute(q_msg[d : d + 1], G, route))
+    block = jnp.concatenate(got, axis=0)
+    blocks = [block]
+    for d in range(1, count_c):
+        route = [(i, i ^ d) for i in range(count_c)]
+        blocks.append(lax.ppermute(block, C, route))
+    q_same, q_swap = pl.pallas_call(
+        spread_kernel,
+        out_shape=(jax.ShapeDtypeStruct((PER, 8 * peers_q, 128), bf16),) * 2,
+        name="spread",
+    )(*blocks)
     parts = pl.pallas_call(
         attend_kernel,
-        out_shape=jax.ShapeDtypeStruct((GROUPS * count_c, 8 * PER + 8, 128), bf16),
+        out_shape=jax.ShapeDtypeStruct((peers_q, 8 * PER + 8, 128), bf16),
+        in_specs=[smem, vmem, vmem, vmem],
         name="attend",
-    )(q_got, kv_got)
+    )(place, q_same, q_swap, kv_got)
     parts_got = lax.all_to_all(parts, G + C, 0, 0, tiled=True)
     change = pl.pallas_call(
         merge_kernel, out_shape=jax.ShapeDtypeStruct((16, DH), f32), name="merge"

time: 109 us -> 121 us (1.11)
  the two profiles are of different devices: /device:TPU:64 before, /device:TPU:1 now
where the time goes in v2:
time: 121 us; the launch traced here: 120 us
  starting transfers between devices  59.2 us (49%)
  waiting for transfers between devices  34.7 us (29%)
  Pallas kernels  14 us (12%)
  local copies, waits for them, and re-layouts  5.88 us (5%)
  other arithmetic  3.24 us (3%)
  between operations  3.01 us (2%)
    ppermute x7, starting transfers between devices, on_device(): blocks.append(lax.ppermute(block, C, route))  25.7 us
    ppermute x3, waiting for transfers between devices, on_device(): got.append(lax.ppermute(q_msg[d:d + 1], G, route))  17.6 us
    all_to_all x1, starting transfers between devices, on_device(): kv_got = lax.all_to_all(kv_msg, G + R, 0, 0, tiled=True)  16.7 us
    all_to_all x1, waiting for transfers between devices, on_device(): parts_got = lax.all_to_all(parts, G + C, 0, 0, tiled=True)  9.31 us
    ppermute x3, starting transfers between devices, on_device(): got.append(lax.ppermute(q_msg[d:d + 1], G, route))  7.85 us
    all_to_all x1, starting transfers between devices, on_device(): parts_got = lax.all_to_all(parts, G + C, 0, 0, tiled=True)  6.75 us
    ppermute x7, waiting for transfers between devices, on_device(): blocks.append(lax.ppermute(block, C, route))  6.37 us
    pallas_call x1, Pallas kernels, on_device(): pl.pallas_call(attend_kernel, out_shape=jax.ShapeDtypeStruct((peers_q, 8...  5.55 us
  transfers between devices with their start and end apart: 13, of which 5 were waited for; matrix products, arithmetic and copies ran while one was open for 2% of the time, Pallas kernels for 3%

profile of v2, /device:TPU:1, one launch (start us, length us, event | category | flops | bytes accessed | tf_op | source)
XLA Modules:
  0.0 120.0 jit_solution(13523068734018679014)
XLA Ops:
  1.9 0.0 copy-start.13
  2.0 0.0 copy-start.14
  2.0 0.6 copy-done.13
  2.6 0.0 copy-done.14
  2.6 0.6 maximum_maximum_fusion.refs_4_
  3.3 2.3 %pack_keys.1 = bf16[32,80,128]{2,1,0:T(8,128)(2,1)} custom-call(bf16[12,1216]{1,0:T(8,128)(2,1)} %bitcast.20, bf16[12,1216]{1,0:T(8,128)(2,1)} %bitcast.21, bf16[1,1216]{1,0:T(2,128)(2,1)} %bitcast.23, bf16[1,1216]{1,0:T(2,128)(2,1)} %bitcast.24, f32[2,128]{1,0:T(2,128)} %maximum_maximum_fusion.refs_4_, s32[1,1]{1,0:T(1,128)} %bitcast.15.refs_5_), custom_call_target="tpu_custom_call" | custom-call | tf_op jit(solution)/shard_map/pack_keys/pallas_call | solution.py:249
  5.6 16.7 %all-to-all-start = ((bf16[32,80,128]{2,1,0:T(8,128)(2,1)}), bf16[32,80,128]{2,1,0:T(8,128)(2,1)S(1)}, u32[]{:S(2)}, u32[]{:S(2)}) async-start(bf16[32,80,128]{2,1,0:T(8,128)(2,1)} %pack_keys.1), calls=%async_computation | async-start | bytes 1310720 | tf_op jit(solution)/shard_map/all_to_all | solution.py:255
  22.3 0.0 copy-start.15
  22.3 0.6 copy-done.15
  23.0 0.6 maximum_bitcast_fusion.gains
  23.6 0.6 pad_add_fusion.place
  24.2 1.7 %pack_queries.1 = bf16[4,40,128]{2,1,0:T(8,128)(2,1)} custom-call(s32[2]{0:T(128)} %pad_add_fusion.place, bf16[12,1216]{1,0:T(8,128)(2,1)} %bitcast.22, f32[1,128]{1,0:T(1,128)} %maximum_bitcast_fusion.gains), custom_call_target="tpu_custom_call" | custom-call | tf_op jit(solution)/shard_map/pack_queries/pallas_call | solution.py:256
  25.9 0.8 fusion
  26.7 2.1 %collective-permute-start = (bf16[1,40,128]{2,1,0:T(8,128)(2,1)S(1)}, bf16[1,40,128]{2,1,0:T(8,128)(2,1)S(1)}, u32[]{:S(2)}, u32[]{:S(2)}) collective-permute-start(bf16[1,40,128]{2,1,0:T(8,128)(2,1)S(1)} %get-tuple-element.11), channel_id=1, source_target_pairs={{0,1},{1,0},{2,3},{3,2},{4,5},{5,4},{6,7},{7,6},{8,9},{9,8},{10,11... | collective-permute-start | bytes 30728 | tf_op jit(solution)/shard_map/ppermute | solution.py:265
  28.8 3.4 %collective-permute-start.1 = (bf16[1,40,128]{2,1,0:T(8,128)(2,1)S(1)}, bf16[1,40,128]{2,1,0:T(8,128)(2,1)S(1)}, u32[]{:S(2)}, u32[]{:S(2)}) collective-permute-start(bf16[1,40,128]{2,1,0:T(8,128)(2,1)S(1)} %get-tuple-element.10), channel_id=1, source_target_pairs={{0,2},{1,3},{2,0},{3,1},{4,6},{5,7},{6,4},{7,5},{8,10},{9,11},{10,... | collective-permute-start | bytes 30728 | tf_op jit(solution)/shard_map/ppermute | solution.py:265
  32.2 2.3 %collective-permute-start.2 = (bf16[1,40,128]{2,1,0:T(8,128)(2,1)S(1)}, bf16[1,40,128]{2,1,0:T(8,128)(2,1)S(1)}, u32[]{:S(2)}, u32[]{:S(2)}) collective-permute-start(bf16[1,40,128]{2,1,0:T(8,128)(2,1)S(1)} %get-tuple-element.9), channel_id=1, source_target_pairs={{0,3},{1,2},{2,1},{3,0},{4,7},{5,6},{6,5},{7,4},{8,11},{9,10},{10,... | collective-permute-start | bytes 30728 | tf_op jit(solution)/shard_map/ppermute | solution.py:265
  34.5 0.0 collective-permute-done
  34.5 15.0 %collective-permute-done.1 = bf16[1,40,128]{2,1,0:T(8,128)(2,1)S(1)} collective-permute-done((bf16[1,40,128]{2,1,0:T(8,128)(2,1)S(1)}, bf16[1,40,128]{2,1,0:T(8,128)(2,1)S(1)}, u32[]{:S(2)}, u32[]{:S(2)}) %collective-permute-start.1) | collective-permute-done | bytes 10272 | tf_op jit(solution)/shard_map/ppermute | solution.py:265
  49.6 2.5 %collective-permute-done.2 = bf16[1,40,128]{2,1,0:T(8,128)(2,1)S(1)} collective-permute-done((bf16[1,40,128]{2,1,0:T(8,128)(2,1)S(1)}, bf16[1,40,128]{2,1,0:T(8,128)(2,1)S(1)}, u32[]{:S(2)}, u32[]{:S(2)}) %collective-permute-start.2) | collective-permute-done | bytes 10272 | tf_op jit(solution)/shard_map/ppermute | solution.py:265
  52.1 0.0 copy-start.2
  52.1 4.7 %collective-permute-start.3 = (bf16[4,40,128]{2,1,0:T(8,128)(2,1)S(1)}, bf16[4,40,128]{2,1,0:T(8,128)(2,1)S(1)}, u32[]{:S(2)}, u32[]{:S(2)}) collective-permute-start(bf16[4,40,128]{2,1,0:T(8,128)(2,1)S(1)} %pad_maximum_fusion.refs_0_), channel_id=1, source_target_pairs={{0,32},{32,0},{64,96},{96,64},{128,160},{160,128},{192,224},{224,1... | collective-permute-start | bytes 122888 | tf_op jit(solution)/shard_map/ppermute | solution.py:270
  56.8 3.2 %collective-permute-start.4 = (bf16[4,40,128]{2,1,0:T(8,128)(2,1)S(1)}, bf16[4,40,128]{2,1,0:T(8,128)(2,1)S(1)}, u32[]{:S(2)}, u32[]{:S(2)}) collective-permute-start(bf16[4,40,128]{2,1,0:T(8,128)(2,1)S(1)} %pad_maximum_fusion.refs_0_), channel_id=1, source_target_pairs={{0,64},{32,96},{64,0},{96,32},{128,192},{160,224},{192,128},{224,1... | collective-permute-start | bytes 122888 | tf_op jit(solution)/shard_map/ppermute | solution.py:270
  60.0 2.0 %collective-permute-start.5 = (bf16[4,40,128]{2,1,0:T(8,128)(2,1)S(1)}, bf16[4,40,128]{2,1,0:T(8,128)(2,1)S(1)}, u32[]{:S(2)}, u32[]{:S(2)}) collective-permute-start(bf16[4,40,128]{2,1,0:T(8,128)(2,1)S(1)} %pad_maximum_fusion.refs_0_), channel_id=1, source_target_pairs={{0,96},{32,64},{64,32},{96,0},{128,224},{160,192},{192,160},{224,1... | collective-permute-start | bytes 122888 | tf_op jit(solution)/shard_map/ppermute | solution.py:270
  62.0 4.8 %collective-permute-start.6 = (bf16[4,40,128]{2,1,0:T(8,128)(2,1)S(1)}, bf16[4,40,128]{2,1,0:T(8,128)(2,1)S(1)}, u32[]{:S(2)}, u32[]{:S(2)}) collective-permute-start(bf16[4,40,128]{2,1,0:T(8,128)(2,1)S(1)} %pad_maximum_fusion.refs_0_), channel_id=1, source_target_pairs={{0,128},{32,160},{64,192},{96,224},{128,0},{160,32},{192,64},{224,... | collective-permute-start | bytes 122888 | tf_op jit(solution)/shard_map/ppermute | solution.py:270
  66.9 4.4 %collective-permute-start.7 = (bf16[4,40,128]{2,1,0:T(8,128)(2,1)S(1)}, bf16[4,40,128]{2,1,0:T(8,128)(2,1)S(1)}, u32[]{:S(2)}, u32[]{:S(2)}) collective-permute-start(bf16[4,40,128]{2,1,0:T(8,128)(2,1)S(1)} %pad_maximum_fusion.refs_0_), channel_id=1, source_target_pairs={{0,160},{32,128},{64,224},{96,192},{128,32},{160,0},{192,96},{224,... | collective-permute-start | bytes 122888 | tf_op jit(solution)/shard_map/ppermute | solution.py:270
  71.3 0.0 collective-permute-done.3.refs_1_
  71.3 0.0 copy-start.4
  71.3 4.6 %collective-permute-start.8 = (bf16[4,40,128]{2,1,0:T(8,128)(2,1)S(1)}, bf16[4,40,128]{2,1,0:T(8,128)(2,1)S(1)}, u32[]{:S(2)}, u32[]{:S(2)}) collective-permute-start(bf16[4,40,128]{2,1,0:T(8,128)(2,1)S(1)} %pad_maximum_fusion.refs_0_), channel_id=1, source_target_pairs={{0,192},{32,224},{64,128},{96,160},{128,64},{160,96},{192,0},{224,... | collective-permute-start | bytes 122888 | tf_op jit(solution)/shard_map/ppermute | solution.py:270
  76.0 0.0 collective-permute-done.4.refs_2_
  76.0 0.0 copy-start.5
  76.0 1.9 %collective-permute-start.9 = (bf16[4,40,128]{2,1,0:T(8,128)(2,1)S(1)}, bf16[4,40,128]{2,1,0:T(8,128)(2,1)S(1)}, u32[]{:S(2)}, u32[]{:S(2)}) collective-permute-start(bf16[4,40,128]{2,1,0:T(8,128)(2,1)S(1)} %pad_maximum_fusion.refs_0_), channel_id=1, source_target_pairs={{0,224},{32,192},{64,160},{96,128},{128,96},{160,64},{192,32},{224... | collective-permute-start | bytes 122888 | tf_op jit(solution)/shard_map/ppermute | solution.py:270
  77.9 0.0 collective-permute-done.5.refs_3_
  77.9 0.0 copy-start.6
  77.9 0.0 collective-permute-done.6.refs_4_
  77.9 0.0 copy-start.7
  77.9 0.0 collective-permute-done.7.refs_5_
  78.0 0.0 copy-start.8
  78.0 0.0 collective-permute-done.8.refs_6_
  78.0 0.0 copy-start.9
  78.0 6.3 %collective-permute-done.9.refs_7_ = bf16[4,40,128]{2,1,0:T(8,128)(2,1)S(1)} collective-permute-done((bf16[4,40,128]{2,1,0:T(8,128)(2,1)S(1)}, bf16[4,40,128]{2,1,0:T(8,128)(2,1)S(1)}, u32[]{:S(2)}, u32[]{:S(2)}) %collective-permute-start.9) | collective-permute-done | bytes 40992 | tf_op jit(solution)/shard_map/ppermute | solution.py:270
  84.3 0.0 copy-done.2
  84.3 0.0 copy-done.4
  84.3 0.0 copy-done.5
  84.3 0.0 copy-done.6
  84.4 0.0 copy-done.7
  84.4 0.6 copy-done.10
  85.0 1.8 %spread.1 = (bf16[5,256,128]{2,1,0:T(8,128)(2,1)}, bf16[5,256,128]{2,1,0:T(8,128)(2,1)}) custom-call(bf16[4,40,128]{2,1,0:T(8,128)(2,1)} %copy-done.2, bf16[4,40,128]{2,1,0:T(8,128)(2,1)} %copy-done.4, bf16[4,40,128]{2,1,0:T(8,128)(2,1)} %copy-done.5, bf16[4,40,128]{2,1,0:T(8,128)(2,1)} %copy-done.6, bf16[4,40,128]{2,1,0:T(8,128)(2,1)} %copy-done.7, ...), custom_call_target="tpu_custom_call" | custom-call | tf_op jit(solution)/shard_map/spread/pallas_call | solution.py:271
  86.8 0.0 all-to-all-done.kv_in
  86.8 0.8 copy-done
  87.7 5.6 %attend.1 = bf16[32,48,128]{2,1,0:T(8,128)(2,1)} custom-call(s32[2]{0:T(128)} %pad_add_fusion.place, bf16[5,256,128]{2,1,0:T(8,128)(2,1)} %get-tuple-element.4.same, bf16[5,256,128]{2,1,0:T(8,128)(2,1)} %get-tuple-element.5.other, bf16[32,80,128]{2,1,0:T(8,128)(2,1)} %copy-done), custom_call_target="tpu_custom_call" | custom-call | tf_op jit(solution)/shard_map/attend/pallas_call | solution.py:276
  93.2 6.8 %all-to-all-start.1 = ((bf16[32,48,128]{2,1,0:T(8,128)(2,1)}), bf16[32,48,128]{2,1,0:T(8,128)(2,1)S(1)}, u32[]{:S(2)}, u32[]{:S(2)}) async-start(bf16[32,48,128]{2,1,0:T(8,128)(2,1)} %attend.1), calls=%async_computation.1 | async-start | bytes 786432 | tf_op jit(solution)/shard_map/all_to_all | solution.py:282
  100.0 0.9 copy.16.weight
  100.9 9.3 %all-to-all-done.1.parts_in = bf16[32,48,128]{2,1,0:T(8,128)(2,1)S(1)} async-done(((bf16[32,48,128]{2,1,0:T(8,128)(2,1)}), bf16[32,48,128]{2,1,0:T(8,128)(2,1)S(1)}, u32[]{:S(2)}, u32[]{:S(2)}) %all-to-all-start.1) | async-done | bytes 393248 | tf_op jit(solution)/shard_map/all_to_all | solution.py:282
  110.2 0.7 copy-done.1
  110.9 2.6 %merge.1 = f32[16,64]{1,0:T(8,128)} custom-call(bf16[32,48,128]{2,1,0:T(8,128)(2,1)} %copy-done.1, bf16[1216,64]{1,0:T(8,128)(2,1)} %copy.16.weight), custom_call_target="tpu_custom_call" | custom-call | tf_op jit(solution)/shard_map/merge/pallas_call | solution.py:283
  113.5 0.7 fusion.1
  114.2 0.0 copy-done.12
  114.3 0.1 slice_select_fusion
  114.3 2.2 %collective-permute-start.10 = (f32[12,32]{1,0:T(8,128)S(1)}, f32[12,32]{1,0:T(8,128)S(1)}, u32[]{:S(2)}, u32[]{:S(2)}) collective-permute-start(f32[12,32]{1,0:T(8,128)S(1)} %slice_select_fusion), channel_id=1, source_target_pairs={{0,256},{256,0},{1,257},{257,1},{2,258},{258,2},{3,259},{259,3},{4... | collective-permute-start | bytes 4616 | tf_op jit(solution)/shard_map/ppermute | solution.py:292
  117.2 0.0 copy-start.11
  117.3 1.4 %collective-permute-done.10 = f32[12,32]{1,0:T(8,128)S(1)} collective-permute-done((f32[12,32]{1,0:T(8,128)S(1)}, f32[12,32]{1,0:T(8,128)S(1)}, u32[]{:S(2)}, u32[]{:S(2)}) %collective-permute-start.10) | collective-permute-done | bytes 1568 | tf_op jit(solution)/shard_map/ppermute | solution.py:292
  118.7 0.0 copy-done.11
  118.7 0.7 multiply_subtract_fusion
  119.4 0.6 multiply_add_fusion
  (10 shorter events, 0.0 us)
Async XLA Ops:
  1.9 0.7 copy-start.13
  2.0 0.7 copy-start.14
  5.6 81.3 %all-to-all-start = ((bf16[32,80,128]{2,1,0:T(8,128)(2,1)}), bf16[32,80,128]{2,1,0:T(8,128)(2,1)S(1)}, u32[]{:S(2)}, u32[]{:S(2)}) async-start(bf16[32,80,128]{2,1,0:T(8,128)(2,1)} %pack_keys.1), calls=%async_computation | async-start | bytes 1310720 | tf_op jit(solution)/shard_map/all_to_all | solution.py:255
  22.3 0.7 copy-start.15
  26.7 7.9 %collective-permute-start = (bf16[1,40,128]{2,1,0:T(8,128)(2,1)S(1)}, bf16[1,40,128]{2,1,0:T(8,128)(2,1)S(1)}, u32[]{:S(2)}, u32[]{:S(2)}) collective-permute-start(bf16[1,40,128]{2,1,0:T(8,128)(2,1)S(1)} %get-tuple-element.11), channel_id=1, source_target_pairs={{0,1},{1,0},{2,3},{3,2},{4,5},{5,4},{6,7},{7,6},{8,9},{9,8},{10,11... | collective-permute-start | bytes 30728 | tf_op jit(solution)/shard_map/ppermute | solution.py:265
  28.8 20.8 %collective-permute-start.1 = (bf16[1,40,128]{2,1,0:T(8,128)(2,1)S(1)}, bf16[1,40,128]{2,1,0:T(8,128)(2,1)S(1)}, u32[]{:S(2)}, u32[]{:S(2)}) collective-permute-start(bf16[1,40,128]{2,1,0:T(8,128)(2,1)S(1)} %get-tuple-element.10), channel_id=1, source_target_pairs={{0,2},{1,3},{2,0},{3,1},{4,6},{5,7},{6,4},{7,5},{8,10},{9,11},{10,... | collective-permute-start | bytes 30728 | tf_op jit(solution)/shard_map/ppermute | solution.py:265
  32.2 19.9 %collective-permute-start.2 = (bf16[1,40,128]{2,1,0:T(8,128)(2,1)S(1)}, bf16[1,40,128]{2,1,0:T(8,128)(2,1)S(1)}, u32[]{:S(2)}, u32[]{:S(2)}) collective-permute-start(bf16[1,40,128]{2,1,0:T(8,128)(2,1)S(1)} %get-tuple-element.9), channel_id=1, source_target_pairs={{0,3},{1,2},{2,1},{3,0},{4,7},{5,6},{6,5},{7,4},{8,11},{9,10},{10,... | collective-permute-start | bytes 30728 | tf_op jit(solution)/shard_map/ppermute | solution.py:265
  52.1 32.2 %copy-start.2 = (bf16[4,40,128]{2,1,0:T(8,128)(2,1)}, bf16[4,40,128]{2,1,0:T(8,128)(2,1)S(1)}, u32[]{:S(2)}) copy-start(bf16[4,40,128]{2,1,0:T(8,128)(2,1)S(1)} %pad_maximum_fusion.refs_0_) | copy-start | bytes 122884
  52.1 19.2 %collective-permute-start.3 = (bf16[4,40,128]{2,1,0:T(8,128)(2,1)S(1)}, bf16[4,40,128]{2,1,0:T(8,128)(2,1)S(1)}, u32[]{:S(2)}, u32[]{:S(2)}) collective-permute-start(bf16[4,40,128]{2,1,0:T(8,128)(2,1)S(1)} %pad_maximum_fusion.refs_0_), channel_id=1, source_target_pairs={{0,32},{32,0},{64,96},{96,64},{128,160},{160,128},{192,224},{224,1... | collective-permute-start | bytes 122888 | tf_op jit(solution)/shard_map/ppermute | solution.py:270
  56.8 19.2 %collective-permute-start.4 = (bf16[4,40,128]{2,1,0:T(8,128)(2,1)S(1)}, bf16[4,40,128]{2,1,0:T(8,128)(2,1)S(1)}, u32[]{:S(2)}, u32[]{:S(2)}) collective-permute-start(bf16[4,40,128]{2,1,0:T(8,128)(2,1)S(1)} %pad_maximum_fusion.refs_0_), channel_id=1, source_target_pairs={{0,64},{32,96},{64,0},{96,32},{128,192},{160,224},{192,128},{224,1... | collective-permute-start | bytes 122888 | tf_op jit(solution)/shard_map/ppermute | solution.py:270
  60.0 17.9 %collective-permute-start.5 = (bf16[4,40,128]{2,1,0:T(8,128)(2,1)S(1)}, bf16[4,40,128]{2,1,0:T(8,128)(2,1)S(1)}, u32[]{:S(2)}, u32[]{:S(2)}) collective-permute-start(bf16[4,40,128]{2,1,0:T(8,128)(2,1)S(1)} %pad_maximum_fusion.refs_0_), channel_id=1, source_target_pairs={{0,96},{32,64},{64,32},{96,0},{128,224},{160,192},{192,160},{224,1... | collective-permute-start | bytes 122888 | tf_op jit(solution)/shard_map/ppermute | solution.py:270
  62.0 15.9 %collective-permute-start.6 = (bf16[4,40,128]{2,1,0:T(8,128)(2,1)S(1)}, bf16[4,40,128]{2,1,0:T(8,128)(2,1)S(1)}, u32[]{:S(2)}, u32[]{:S(2)}) collective-permute-start(bf16[4,40,128]{2,1,0:T(8,128)(2,1)S(1)} %pad_maximum_fusion.refs_0_), channel_id=1, source_target_pairs={{0,128},{32,160},{64,192},{96,224},{128,0},{160,32},{192,64},{224,... | collective-permute-start | bytes 122888 | tf_op jit(solution)/shard_map/ppermute | solution.py:270
  66.9 11.1 %collective-permute-start.7 = (bf16[4,40,128]{2,1,0:T(8,128)(2,1)S(1)}, bf16[4,40,128]{2,1,0:T(8,128)(2,1)S(1)}, u32[]{:S(2)}, u32[]{:S(2)}) collective-permute-start(bf16[4,40,128]{2,1,0:T(8,128)(2,1)S(1)} %pad_maximum_fusion.refs_0_), channel_id=1, source_target_pairs={{0,160},{32,128},{64,224},{96,192},{128,32},{160,0},{192,96},{224,... | collective-permute-start | bytes 122888 | tf_op jit(solution)/shard_map/ppermute | solution.py:270
  71.3 13.0 %copy-start.4 = (bf16[4,40,128]{2,1,0:T(8,128)(2,1)}, bf16[4,40,128]{2,1,0:T(8,128)(2,1)S(1)}, u32[]{:S(2)}) copy-start(bf16[4,40,128]{2,1,0:T(8,128)(2,1)S(1)} %collective-permute-done.3.refs_1_) | copy-start | bytes 122884
  71.3 6.7 %collective-permute-start.8 = (bf16[4,40,128]{2,1,0:T(8,128)(2,1)S(1)}, bf16[4,40,128]{2,1,0:T(8,128)(2,1)S(1)}, u32[]{:S(2)}, u32[]{:S(2)}) collective-permute-start(bf16[4,40,128]{2,1,0:T(8,128)(2,1)S(1)} %pad_maximum_fusion.refs_0_), channel_id=1, source_target_pairs={{0,192},{32,224},{64,128},{96,160},{128,64},{160,96},{192,0},{224,... | collective-permute-start | bytes 122888 | tf_op jit(solution)/shard_map/ppermute | solution.py:270
  76.0 8.4 %copy-start.5 = (bf16[4,40,128]{2,1,0:T(8,128)(2,1)}, bf16[4,40,128]{2,1,0:T(8,128)(2,1)S(1)}, u32[]{:S(2)}) copy-start(bf16[4,40,128]{2,1,0:T(8,128)(2,1)S(1)} %collective-permute-done.4.refs_2_) | copy-start | bytes 122884
  76.0 8.4 %collective-permute-start.9 = (bf16[4,40,128]{2,1,0:T(8,128)(2,1)S(1)}, bf16[4,40,128]{2,1,0:T(8,128)(2,1)S(1)}, u32[]{:S(2)}, u32[]{:S(2)}) collective-permute-start(bf16[4,40,128]{2,1,0:T(8,128)(2,1)S(1)} %pad_maximum_fusion.refs_0_), channel_id=1, source_target_pairs={{0,224},{32,192},{64,160},{96,128},{128,96},{160,64},{192,32},{224... | collective-permute-start | bytes 122888 | tf_op jit(solution)/shard_map/ppermute | solution.py:270
  77.9 6.4 %copy-start.6 = (bf16[4,40,128]{2,1,0:T(8,128)(2,1)}, bf16[4,40,128]{2,1,0:T(8,128)(2,1)S(1)}, u32[]{:S(2)}) copy-start(bf16[4,40,128]{2,1,0:T(8,128)(2,1)S(1)} %collective-permute-done.5.refs_3_) | copy-start | bytes 122884
  77.9 6.4 %copy-start.7 = (bf16[4,40,128]{2,1,0:T(8,128)(2,1)}, bf16[4,40,128]{2,1,0:T(8,128)(2,1)S(1)}, u32[]{:S(2)}) copy-start(bf16[4,40,128]{2,1,0:T(8,128)(2,1)S(1)} %collective-permute-done.6.refs_4_) | copy-start | bytes 122884
  78.0 6.4 %copy-start.8 = (bf16[4,40,128]{2,1,0:T(8,128)(2,1)}, bf16[4,40,128]{2,1,0:T(8,128)(2,1)S(1)}, u32[]{:S(2)}) copy-start(bf16[4,40,128]{2,1,0:T(8,128)(2,1)S(1)} %collective-permute-done.7.refs_5_) | copy-start | bytes 122884
  78.0 6.4 %copy-start.9 = (bf16[4,40,128]{2,1,0:T(8,128)(2,1)}, bf16[4,40,128]{2,1,0:T(8,128)(2,1)S(1)}, u32[]{:S(2)}) copy-start(bf16[4,40,128]{2,1,0:T(8,128)(2,1)S(1)} %collective-permute-done.8.refs_6_) | copy-start | bytes 122884
  84.4 0.6 copy-start.10
  86.8 0.8 copy-start
  93.2 6.8 %copy-start.3 = (bf16[1216,64]{0,1:T(8,128)(2,1)S(1)}, bf16[1216,64]{0,1:T(8,128)(2,1)}, u32[]{:S(2)}) copy-start(bf16[1216,64]{0,1:T(8,128)(2,1)} %param.26) | copy-start | bytes 466948
  93.2 17.0 %all-to-all-start.1 = ((bf16[32,48,128]{2,1,0:T(8,128)(2,1)}), bf16[32,48,128]{2,1,0:T(8,128)(2,1)S(1)}, u32[]{:S(2)}, u32[]{:S(2)}) async-start(bf16[32,48,128]{2,1,0:T(8,128)(2,1)} %attend.1), calls=%async_computation.1 | async-start | bytes 786432 | tf_op jit(solution)/shard_map/all_to_all | solution.py:282
  110.2 0.7 copy-start.1
  113.5 0.7 copy-start.12
  114.3 4.4 %collective-permute-start.10 = (f32[12,32]{1,0:T(8,128)S(1)}, f32[12,32]{1,0:T(8,128)S(1)}, u32[]{:S(2)}, u32[]{:S(2)}) collective-permute-start(f32[12,32]{1,0:T(8,128)S(1)} %slice_select_fusion), channel_id=1, source_target_pairs={{0,256},{256,0},{1,257},{257,1},{2,258},{258,2},{3,259},{259,3},{4... | collective-permute-start | bytes 4616 | tf_op jit(solution)/shard_map/ppermute | solution.py:292
  117.2 1.5 %copy-start.11 = (f32[12,32]{1,0:T(8,128)S(1)}, f32[12,32]{1,0:T(8,128)}, u32[]{:S(2)}) copy-start(f32[12,32]{1,0:T(8,128)} %param.24) | copy-start | bytes 4612

commit v3 on v2

--- a/solution.py
+++ b/solution.py
@@ -30,6 +30,10 @@
 def sigma_at(position):
     time_left = 1.0 - position / STEPS
     return shift_factor * time_left / (1.0 + (shift_factor - 1.0) * time_left)
+
+
+def near(x):
+    return pltpu.with_memory_space_constraint(x, pltpu.VMEM)
 
 
 def left_lanes(shape):
@@ -101,7 +105,7 @@
     send_copies(out, copies, heads)
 
 
-def pack_queries(place, q, gains, out):
+def pack_queries(q, gains, out):
     zero = jnp.zeros((2, 128), f32)
     heads = []
 
@@ -111,17 +115,19 @@
     head_tiles((q,), (gains[...],), add)
     for g in range(GROUPS):
         message = jnp.concatenate(heads[PER * g : PER * (g + 1)], axis=0).astype(bf16)
-        out[jnp.bitwise_xor(place[0], g)] = message
+        out[g] = message
 
 
 def spread_kernel(*refs):
     *blocks, same, other = refs
-    rows = 8 * GROUPS
-    for d, block in enumerate(blocks):
+    start = 0
+    for block in blocks:
+        rows = 8 * block.shape[0]
         for j in range(PER):
             q = rows_of(block[:, 8 * j : 8 * j + 8, :].astype(f32))
-            same[j, rows * d : rows * (d + 1), :] = q.astype(bf16)
-            other[j, rows * d : rows * (d + 1), :] = swap(q).astype(bf16)
+            same[j, start : start + rows, :] = q.astype(bf16)
+            other[j, start : start + rows, :] = swap(q).astype(bf16)
+        start += rows
 
 
 def rows_of(block):
@@ -132,7 +138,7 @@
     return lax.dot_general(a, b, (((1,), (1,)), ((), ())), preferred_element_type=f32)
 
 
-def attend_kernel(place, same, other, kv_in, out):
+def attend_kernel(offsets, place, same, other, kv_in, out):
     peers_q = same.shape[1] // 8
     peers_k = kv_in.shape[0]
     keys = peers_k * 8
@@ -185,12 +191,12 @@
     for j in range(0, PER + 1, 2):
         pair = jnp.concatenate([tiles[j], tiles[j + 1]], axis=1).astype(bf16)
         for b in range(peers_q):
-            owner = jnp.bitwise_xor(place[0], b % GROUPS) * (peers_q // GROUPS)
-            owner += jnp.bitwise_xor(place[1], b // GROUPS)
+            owner = jnp.bitwise_xor(place[0], offsets[b // GROUPS])
+            owner += b % GROUPS * len(offsets)
             out[owner, 8 * j : 8 * j + 16, :] = pair[b]
 
 
-def merge_kernel(parts_in, weight, out):
+def merge_kernel(half, parts_in, weight, base, own_out, sent_out):
     blocks = parts_in.shape[0] // GROUPS
     left = left_lanes((blocks, 8, 128))
     left8 = left_lanes((8, 128))
@@ -217,7 +223,11 @@
             total += jnp.dot(
                 both, jnp.concatenate([rows, rows], axis=0), preferred_element_type=f32
             )
-    out[...] = total
+    change = jnp.concatenate([total[:HALF], total[8 : 8 + HALF]], axis=0)
+    velocity = base[...].astype(f32) + change
+    low, high = velocity[:, : DH // 2], velocity[:, DH // 2 :]
+    own_out[...] = jnp.where(half[0] == 0, low, high)
+    sent_out[...] = jnp.where(half[0] == 0, high, low)
 
 
 def on_device(
@@ -245,7 +255,13 @@
     twice = jnp.concatenate([jnp.stack([key_gain, text_gain])] * 2, axis=1)
     query_twice = jnp.concatenate([query_gain, query_gain]).reshape(1, 2 * DH)
     peers_q = GROUPS * count_c
-    place = jnp.stack([lax.axis_index(G), lax.axis_index(C)])
+    place = lax.axis_index(C).reshape(1)
+    q_msg = pl.pallas_call(
+        pack_queries,
+        out_shape=jax.ShapeDtypeStruct((GROUPS, 8 * PER, 128), bf16),
+        name="pack_queries",
+    )(img_queries[0], query_twice)
+    block = lax.all_to_all(q_msg, G, 0, 0, tiled=True)
     kv_msg = pl.pallas_call(
         lambda *refs: pack_keys(count_r, *refs),
         out_shape=jax.ShapeDtypeStruct((GROUPS * count_r, 16 * PER, 128), bf16),
@@ -253,42 +269,39 @@
         name="pack_keys",
     )(img_keys[0], img_values[0], text_keys[0], text_values[0], twice, usable.reshape(1, 1))
     kv_got = lax.all_to_all(kv_msg, G + R, 0, 0, tiled=True)
-    q_msg = pl.pallas_call(
-        pack_queries,
-        out_shape=jax.ShapeDtypeStruct((GROUPS, 8 * PER, 128), bf16),
-        in_specs=[smem, vmem, vmem],
-        name="pack_queries",
-    )(place, img_queries[0], query_twice)
-    got = [q_msg[:1]]
-    for d in range(1, GROUPS):
-        route = [(i, i ^ d) for i in range(GROUPS)]
-        got.append(lax.ppermute(q_msg[d : d + 1], G, route))
-    block = jnp.concatenate(got, axis=0)
     blocks = [block]
-    for d in range(1, count_c):
-        route = [(i, i ^ d) for i in range(count_c)]
-        blocks.append(lax.ppermute(block, C, route))
+    offsets = [0]
+    unit = count_c
+    for axis in C:
+        size = lax.axis_size(axis)
+        unit //= size
+        step = 1
+        while step < size:
+            block = jnp.concatenate(blocks, axis=0) if len(blocks) > 1 else block
+            route = [(i, i ^ step) for i in range(size)]
+            blocks = [block, lax.ppermute(block, axis, route)]
+            offsets += [o ^ (step * unit) for o in offsets]
+            step *= 2
     q_same, q_swap = pl.pallas_call(
         spread_kernel,
         out_shape=(jax.ShapeDtypeStruct((PER, 8 * peers_q, 128), bf16),) * 2,
         name="spread",
-    )(*blocks)
+    )(*[near(block) for block in blocks])
     parts = pl.pallas_call(
-        attend_kernel,
+        lambda *refs: attend_kernel(offsets, *refs),
         out_shape=jax.ShapeDtypeStruct((peers_q, 8 * PER + 8, 128), bf16),
         in_specs=[smem, vmem, vmem, vmem],
         name="attend",
-    )(place, q_same, q_swap, kv_got)
+    )(place, q_same, q_swap, near(kv_got))
     parts_got = lax.all_to_all(parts, G + C, 0, 0, tiled=True)
-    change = pl.pallas_call(
-        merge_kernel, out_shape=jax.ShapeDtypeStruct((16, DH), f32), name="merge"
-    )(parts_got, out_weight)
-    change = jnp.concatenate([change[:HALF], change[8 : 8 + HALF]], axis=0)
-    velocity = base_velocity[0].astype(f32) + change
     guide_half = lax.axis_index("cfg")
-    width = latent.shape[1]
-    own_part = jnp.where(guide_half == 0, velocity[:, :width], velocity[:, width:])
-    sent_part = jnp.where(guide_half == 0, velocity[:, width:], velocity[:, :width])
+    share = jax.ShapeDtypeStruct(latent.shape, f32)
+    own_part, sent_part = pl.pallas_call(
+        merge_kernel,
+        out_shape=(share, share),
+        in_specs=[smem, vmem, vmem, vmem],
+        name="merge",
+    )(guide_half.reshape(1), near(parts_got), out_weight, base_velocity[0])
     partner = lax.ppermute(sent_part, "cfg", [(0, 1), (1, 0)])
     cond_part = jnp.where(guide_half == 0, own_part, partner)
     uncond_part = jnp.where(guide_half == 0, partner, own_part)

time: 121 us -> 98 us (0.81)
  the two profiles are of different devices: /device:TPU:1 before, /device:TPU:64 now
where the time goes in v3:
time: 98 us; the launch traced here: 97.3 us
  starting transfers between devices  42.2 us (43%)
  waiting for transfers between devices  35.5 us (36%)
  Pallas kernels  12.7 us (13%)
  between operations  2.83 us (3%)
  other arithmetic  2.57 us (3%)
  local copies, waits for them, and re-layouts  1.59 us (2%)
    all_to_all x1, starting transfers between devices, on_device(): kv_got = lax.all_to_all(kv_msg, G + R, 0, 0, tiled=True)  15.4 us
    all_to_all x1, waiting for transfers between devices, on_device(): kv_got = lax.all_to_all(kv_msg, G + R, 0, 0, tiled=True)  13.9 us
    ppermute x3, starting transfers between devices, on_device(): blocks = [block, lax.ppermute(block, axis, route)]  13.5 us
    all_to_all x1, waiting for transfers between devices, on_device(): parts_got = lax.all_to_all(parts, G + C, 0, 0, tiled=True)  10.3 us
    ppermute x3, waiting for transfers between devices, on_device(): blocks = [block, lax.ppermute(block, axis, route)]  8.87 us
    all_to_all x1, starting transfers between devices, on_device(): parts_got = lax.all_to_all(parts, G + C, 0, 0, tiled=True)  7.44 us
    pallas_call x1, Pallas kernels, on_device(): pl.pallas_call(lambda *refs: attend_kernel(offsets, *refs), out_shape=jax...  5.31 us
    all_to_all x1, starting transfers between devices, on_device(): block = lax.all_to_all(q_msg, G, 0, 0, tiled=True)  3.27 us
  transfers between devices with their start and end apart: 7, of which 6 were waited for; matrix products, arithmetic and copies ran while one was open for 2% of the time, Pallas kernels for 3%

profile of v3, /device:TPU:64, one launch (start us, length us, event | category | flops | bytes accessed | tf_op | source)
XLA Modules:
  0.0 97.3 jit_solution(1301596204166952014)
XLA Ops:
  0.6 1.3 %maximum_bitcast_fusion.gains = f32[1,128]{1,0:T(1,128)} fusion(f32[64]{0:T(128)} %param.19), kind=kLoop, calls=%fused_computation.8 | loop fusion | flops 128 | bytes 768 | tf_op jit(solution)/shard_map/reshape | solution.py:256
  1.9 1.6 %pack_queries.1 = bf16[4,40,128]{2,1,0:T(8,128)(2,1)} custom-call(bf16[12,1216]{1,0:T(8,128)(2,1)} %bitcast.20, f32[1,128]{1,0:T(1,128)} %maximum_bitcast_fusion.gains), custom_call_target="tpu_custom_call" | custom-call | tf_op jit(solution)/shard_map/pack_queries/pallas_call | solution.py:259
  3.5 3.3 %all-to-all-start = ((bf16[4,40,128]{2,1,0:T(8,128)(2,1)}), bf16[4,40,128]{2,1,0:T(8,128)(2,1)S(1)}, u32[]{:S(2)}, u32[]{:S(2)}) async-start(bf16[4,40,128]{2,1,0:T(8,128)(2,1)} %pack_queries.1), calls=%async_computation | async-start | bytes 81920 | tf_op jit(solution)/shard_map/all_to_all | solution.py:264
  8.1 0.0 copy-start.3
  8.1 0.0 copy-start.4
  8.2 0.6 copy-done.3
  8.8 0.0 copy-done.4
  8.8 0.6 maximum_maximum_fusion.refs_4_
  9.4 2.3 %pack_keys.1 = bf16[32,80,128]{2,1,0:T(8,128)(2,1)} custom-call(bf16[12,1216]{1,0:T(8,128)(2,1)} %bitcast.18, bf16[12,1216]{1,0:T(8,128)(2,1)} %bitcast.19, bf16[1,1216]{1,0:T(2,128)(2,1)} %bitcast.21, bf16[1,1216]{1,0:T(2,128)(2,1)} %bitcast.22, f32[2,128]{1,0:T(2,128)} %maximum_maximum_fusion.refs_4_, s32[1,1]{1,0:T(1,128)} %bitcast.14.refs_5_), custom_call_target="tpu_custom_call" | custom-call | tf_op jit(solution)/shard_map/pack_keys/pallas_call | solution.py:265
  11.8 0.0 all-to-all-done
  11.8 15.4 %all-to-all-start.1 = ((bf16[32,80,128]{2,1,0:T(8,128)(2,1)}), bf16[32,80,128]{2,1,0:T(8,128)(2,1)S(1)}, u32[]{:S(2)}, u32[]{:S(2)}) async-start(bf16[32,80,128]{2,1,0:T(8,128)(2,1)} %pack_keys.1), calls=%async_computation.1 | async-start | bytes 1310720 | tf_op jit(solution)/shard_map/all_to_all | solution.py:271
  27.2 3.5 %collective-permute-start = (bf16[4,40,128]{2,1,0:T(8,128)(2,1)S(1)}, bf16[4,40,128]{2,1,0:T(8,128)(2,1)S(1)}, u32[]{:S(2)}, u32[]{:S(2)}) collective-permute-start(bf16[4,40,128]{2,1,0:T(8,128)(2,1)S(1)} %all-to-all-done), channel_id=1, source_target_pairs={{0,64},{64,0},{128,192},{192,128},{1,65},{65,1},{129,193},{193,129... | collective-permute-start | bytes 122888 | tf_op jit(solution)/shard_map/ppermute | solution.py:282
  30.7 2.4 %collective-permute-done = bf16[4,40,128]{2,1,0:T(8,128)(2,1)S(1)} collective-permute-done((bf16[4,40,128]{2,1,0:T(8,128)(2,1)S(1)}, bf16[4,40,128]{2,1,0:T(8,128)(2,1)S(1)}, u32[]{:S(2)}, u32[]{:S(2)}) %collective-permute-start) | collective-permute-done | bytes 40992 | tf_op jit(solution)/shard_map/ppermute | solution.py:282
  33.1 5.1 %collective-permute-start.1 = (bf16[8,40,128]{2,1,0:T(8,128)(2,1)S(1)}, bf16[8,40,128]{2,1,0:T(8,128)(2,1)S(1)}, u32[]{:S(2)}, u32[]{:S(2)}) collective-permute-start(bf16[8,40,128]{2,1,0:T(8,128)(2,1)S(1)} %pad_maximum_fusion), channel_id=1, source_target_pairs={{0,128},{64,192},{128,0},{192,64},{1,129},{65,193},{129,1},{193,65... | collective-permute-start | bytes 245768 | tf_op jit(solution)/shard_map/ppermute | solution.py:282
  38.2 2.7 %collective-permute-done.1 = bf16[8,40,128]{2,1,0:T(8,128)(2,1)S(1)} collective-permute-done((bf16[8,40,128]{2,1,0:T(8,128)(2,1)S(1)}, bf16[8,40,128]{2,1,0:T(8,128)(2,1)S(1)}, u32[]{:S(2)}, u32[]{:S(2)}) %collective-permute-start.1) | collective-permute-done | bytes 81952 | tf_op jit(solution)/shard_map/ppermute | solution.py:282
  41.0 4.9 %collective-permute-start.2 = (bf16[16,40,128]{2,1,0:T(8,128)(2,1)S(1)}, bf16[16,40,128]{2,1,0:T(8,128)(2,1)S(1)}, u32[]{:S(2)}, u32[]{:S(2)}) collective-permute-start(bf16[16,40,128]{2,1,0:T(8,128)(2,1)S(1)} %constant_dynamic-update-slice_fusion.refs_0_), channel_id=1, source_target_pairs={{0,32},{32,0},{1,33},{33,1},{2,34},{34,2},{3,35},{35,3},{4,36},{36... | collective-permute-start | bytes 491528 | tf_op jit(solution)/shard_map/ppermute | solution.py:282
  45.9 3.8 %collective-permute-done.2.refs_1_ = bf16[16,40,128]{2,1,0:T(8,128)(2,1)S(1)} collective-permute-done((bf16[16,40,128]{2,1,0:T(8,128)(2,1)S(1)}, bf16[16,40,128]{2,1,0:T(8,128)(2,1)S(1)}, u32[]{:S(2)}, u32[]{:S(2)}) %collective-permute-start.2) | collective-permute-done | bytes 163872 | tf_op jit(solution)/shard_map/ppermute | solution.py:282
  49.7 0.9 spread.1
  50.6 13.9 %all-to-all-done.1.refs_3_ = bf16[32,80,128]{2,1,0:T(8,128)(2,1)S(1)} async-done(((bf16[32,80,128]{2,1,0:T(8,128)(2,1)}), bf16[32,80,128]{2,1,0:T(8,128)(2,1)S(1)}, u32[]{:S(2)}, u32[]{:S(2)}) %all-to-all-start.1) | async-done | bytes 655392 | tf_op jit(solution)/shard_map/all_to_all | solution.py:271
  64.5 5.3 %attend.1 = bf16[32,48,128]{2,1,0:T(8,128)(2,1)} custom-call(s32[1]{0:T(128)} %bitcast.3.refs_0_, bf16[5,256,128]{2,1,0:T(8,128)(2,1)} %get-tuple-element.6.refs_1_, bf16[5,256,128]{2,1,0:T(8,128)(2,1)} %get-tuple-element.7.refs_2_, bf16[32,80,128]{2,1,0:T(8,128)(2,1)S(1)} %all-to-all-done.1.refs_3_), custom_call_target="tpu_custom_call" | custom-call | tf_op jit(solution)/shard_map/attend/pallas_call | solution.py:290
  69.8 0.0 copy-start
  69.8 7.4 %all-to-all-start.2 = ((bf16[32,48,128]{2,1,0:T(8,128)(2,1)}), bf16[32,48,128]{2,1,0:T(8,128)(2,1)S(1)}, u32[]{:S(2)}, u32[]{:S(2)}) async-start(bf16[32,48,128]{2,1,0:T(8,128)(2,1)} %attend.1), calls=%async_computation.2 | async-start | bytes 786432 | tf_op jit(solution)/shard_map/all_to_all | solution.py:296
  77.2 0.0 copy-done
  77.2 0.9 copy.16.weight
  78.1 10.3 %all-to-all-done.2.parts_in = bf16[32,48,128]{2,1,0:T(8,128)(2,1)S(1)} async-done(((bf16[32,48,128]{2,1,0:T(8,128)(2,1)}), bf16[32,48,128]{2,1,0:T(8,128)(2,1)S(1)}, u32[]{:S(2)}, u32[]{:S(2)}) %all-to-all-start.2) | async-done | bytes 393248 | tf_op jit(solution)/shard_map/all_to_all | solution.py:296
  88.4 2.6 %merge.1 = (f32[12,32]{1,0:T(8,128)}, f32[12,32]{1,0:T(8,128)}) custom-call(s32[1]{0:T(128)} %bitcast.2.half, bf16[32,48,128]{2,1,0:T(8,128)(2,1)S(1)} %all-to-all-done.2.parts_in, bf16[1216,64]{1,0:T(8,128)(2,1)} %copy.16.weight, bf16[12,64]{1,0:T(8,128)(2,1)} %bitcast.23), custom_call_target="tpu_custom_call" | custom-call | tf_op jit(solution)/shard_map/merge/pallas_call | solution.py:299
  91.0 2.5 %collective-permute-start.3 = (f32[12,32]{1,0:T(8,128)}, f32[12,32]{1,0:T(8,128)S(1)}, u32[]{:S(2)}, u32[]{:S(2)}) collective-permute-start(f32[12,32]{1,0:T(8,128)} %get-tuple-element.8), channel_id=1, source_target_pairs={{0,256},{256,0},{1,257},{257,1},{2,258},{258,2},{3,259},{259,3},{4... | collective-permute-start | bytes 4616 | tf_op jit(solution)/shard_map/ppermute | solution.py:305
  94.1 0.0 copy-start.2
  94.2 0.0 copy-start.1
  94.3 2.5 %collective-permute-done.3 = f32[12,32]{1,0:T(8,128)S(1)} collective-permute-done((f32[12,32]{1,0:T(8,128)}, f32[12,32]{1,0:T(8,128)S(1)}, u32[]{:S(2)}, u32[]{:S(2)}) %collective-permute-start.3) | collective-permute-done | bytes 1568 | tf_op jit(solution)/shard_map/ppermute | solution.py:305
  96.7 0.0 copy-done.2
  96.7 0.0 copy-done.1
  96.7 0.6 multiply_subtract_fusion
  (4 shorter events, 0.0 us)
Async XLA Ops:
  3.5 8.2 %all-to-all-start = ((bf16[4,40,128]{2,1,0:T(8,128)(2,1)}), bf16[4,40,128]{2,1,0:T(8,128)(2,1)S(1)}, u32[]{:S(2)}, u32[]{:S(2)}) async-start(bf16[4,40,128]{2,1,0:T(8,128)(2,1)} %pack_queries.1), calls=%async_computation | async-start | bytes 81920 | tf_op jit(solution)/shard_map/all_to_all | solution.py:264
  8.1 0.7 copy-start.3
  8.1 0.7 copy-start.4
  11.8 52.7 %all-to-all-start.1 = ((bf16[32,80,128]{2,1,0:T(8,128)(2,1)}), bf16[32,80,128]{2,1,0:T(8,128)(2,1)S(1)}, u32[]{:S(2)}, u32[]{:S(2)}) async-start(bf16[32,80,128]{2,1,0:T(8,128)(2,1)} %pack_keys.1), calls=%async_computation.1 | async-start | bytes 1310720 | tf_op jit(solution)/shard_map/all_to_all | solution.py:271
  27.2 5.9 %collective-permute-start = (bf16[4,40,128]{2,1,0:T(8,128)(2,1)S(1)}, bf16[4,40,128]{2,1,0:T(8,128)(2,1)S(1)}, u32[]{:S(2)}, u32[]{:S(2)}) collective-permute-start(bf16[4,40,128]{2,1,0:T(8,128)(2,1)S(1)} %all-to-all-done), channel_id=1, source_target_pairs={{0,64},{64,0},{128,192},{192,128},{1,65},{65,1},{129,193},{193,129... | collective-permute-start | bytes 122888 | tf_op jit(solution)/shard_map/ppermute | solution.py:282
  33.1 7.8 %collective-permute-start.1 = (bf16[8,40,128]{2,1,0:T(8,128)(2,1)S(1)}, bf16[8,40,128]{2,1,0:T(8,128)(2,1)S(1)}, u32[]{:S(2)}, u32[]{:S(2)}) collective-permute-start(bf16[8,40,128]{2,1,0:T(8,128)(2,1)S(1)} %pad_maximum_fusion), channel_id=1, source_target_pairs={{0,128},{64,192},{128,0},{192,64},{1,129},{65,193},{129,1},{193,65... | collective-permute-start | bytes 245768 | tf_op jit(solution)/shard_map/ppermute | solution.py:282
  41.0 8.7 %collective-permute-start.2 = (bf16[16,40,128]{2,1,0:T(8,128)(2,1)S(1)}, bf16[16,40,128]{2,1,0:T(8,128)(2,1)S(1)}, u32[]{:S(2)}, u32[]{:S(2)}) collective-permute-start(bf16[16,40,128]{2,1,0:T(8,128)(2,1)S(1)} %constant_dynamic-update-slice_fusion.refs_0_), channel_id=1, source_target_pairs={{0,32},{32,0},{1,33},{33,1},{2,34},{34,2},{3,35},{35,3},{4,36},{36... | collective-permute-start | bytes 491528 | tf_op jit(solution)/shard_map/ppermute | solution.py:282
  69.8 7.5 %copy-start = (bf16[1216,64]{0,1:T(8,128)(2,1)S(1)}, bf16[1216,64]{0,1:T(8,128)(2,1)}, u32[]{:S(2)}) copy-start(bf16[1216,64]{0,1:T(8,128)(2,1)} %param.26) | copy-start | bytes 466948
  69.8 18.6 %all-to-all-start.2 = ((bf16[32,48,128]{2,1,0:T(8,128)(2,1)}), bf16[32,48,128]{2,1,0:T(8,128)(2,1)S(1)}, u32[]{:S(2)}, u32[]{:S(2)}) async-start(bf16[32,48,128]{2,1,0:T(8,128)(2,1)} %attend.1), calls=%async_computation.2 | async-start | bytes 786432 | tf_op jit(solution)/shard_map/all_to_all | solution.py:296
  91.0 5.7 %collective-permute-start.3 = (f32[12,32]{1,0:T(8,128)}, f32[12,32]{1,0:T(8,128)S(1)}, u32[]{:S(2)}, u32[]{:S(2)}) collective-permute-start(f32[12,32]{1,0:T(8,128)} %get-tuple-element.8), channel_id=1, source_target_pairs={{0,256},{256,0},{1,257},{257,1},{2,258},{258,2},{3,259},{259,3},{4... | collective-permute-start | bytes 4616 | tf_op jit(solution)/shard_map/ppermute | solution.py:305
  94.1 2.6 %copy-start.2 = (f32[12,32]{1,0:T(8,128)S(1)}, f32[12,32]{1,0:T(8,128)}, u32[]{:S(2)}) copy-start(f32[12,32]{1,0:T(8,128)} %get-tuple-element.9) | copy-start | bytes 4612
  94.2 2.6 %copy-start.1 = (f32[12,32]{1,0:T(8,128)S(1)}, f32[12,32]{1,0:T(8,128)}, u32[]{:S(2)}) copy-start(f32[12,32]{1,0:T(8,128)} %param.24) | copy-start | bytes 4612
